TPU v7x, 128 devices: a whole 4x4x4 slice. The times are simulated.
128 devices in a mesh: freq: 2 (over z_lo), tile: 64 (over z_hi, y, x, core).
Axes of the slice: x: 4, y: 4, z: 4 (z_hi: 2, z_lo: 2; z = z_hi * 2 + z_lo), core: 2. Of those that a mesh axis runs over, the one named last changes fastest.
Arguments:
- residual: float32 [2, 3, 65536], P('freq', None, 'tile'), may hold values from -24 to 24
- row_counts: int32 [64, 256], P('tile'), may hold values from 1 to 16, 1024 in all within a row
- recv_owner: int32 [16384, 1], P('tile'), may hold values from 0 to 63; in each aligned block of 256 rows (0 to 255, 256 to 511, ...) at most 16 rows name the same one
- recv_cell: int32 [16384], P('tile'), may hold values from 0 to 262143
- conductivity: float32 [64, 64, 32, 128], P('tile'), may hold values from 0.5 to 4
- laplace: float32 [2], P('freq'), may hold values from 0.25 to 1
- forward_field: bfloat16 [2, 64, 3, 64, 32, 128], P('freq', 'tile'), may hold values from -6 to 6
Outputs:
- gradient: float32 [64, 64, 32, 128], P(None, 'tile', 'freq')
Inputs may be any that keep to these rules, and one draw needn't show every extreme that they name: `row_counts`: the 256 counts of one tile sum to 1024; some receiver has exactly 16 rows. `recv_owner`: among the receivers of one tile at most 16 share an owner tile, and in some tile exactly 16 do.
All inputs are finite; a program needn't handle non-finite values.
Results may differ from a plain program's by a relative error of at most 0.0003.
Values sent between devices are 32-bit elements; how exact they have to be, the bound alone decides.
A program may use at most 320 MiB of HBM per device.

v0:
```python
import jax
import jax.numpy as jnp
from jax import lax
from jax.sharding import PartitionSpec as P

TY = 4
TZ = 4
SWEEPS = 8


RELAXATION = 0.5


def from_behind(array, axis, by):
    devices = lax.axis_size(axis)
    pairs = [(i, i + by) for i in range(devices) if 0 <= i + by < devices]
    return lax.ppermute(array, axis, pairs)


def forward_step(values, direction):
    upper_cut = [slice(0, -1)] * 3
    lower_cut = [slice(0, -1)] * 3
    upper_cut[direction] = slice(1, None)
    return values[tuple(upper_cut)] - values[tuple(lower_cut)]


def backward_step(values, direction):
    upper_cut = [slice(1, None)] * 3
    lower_cut = [slice(1, None)] * 3
    lower_cut[direction] = slice(0, -1)
    return values[tuple(upper_cut)] - values[tuple(lower_cut)]


def curl_curl(padded):
    field_x, field_y, field_z = (padded[0], padded[1], padded[2])
    swirl_x = forward_step(field_z, 1) - forward_step(field_y, 2)
    swirl_y = forward_step(field_x, 2) - forward_step(field_z, 0)
    swirl_z = forward_step(field_y, 0) - forward_step(field_x, 1)
    return jnp.stack(
        [
            backward_step(swirl_z, 1) - backward_step(swirl_y, 2),
            backward_step(swirl_x, 2) - backward_step(swirl_z, 0),
            backward_step(swirl_y, 0) - backward_step(swirl_x, 1),
        ]
    )


def relax_sweep(padded, source, damping, inside):
    centre = padded[:, 1:-1, 1:-1, 1:-1]
    update = centre + RELAXATION * (source - curl_curl(padded) - damping * centre) / (4.0 + damping)
    return update * inside


def grow_rims(values, rim_width, layout):
    coords, limits, strides = layout
    for direction in range(3):
        extent = values.shape[direction + 1]
        upper_face = lax.slice_in_dim(values, extent - rim_width, extent, axis=direction + 1)
        lower_face = lax.slice_in_dim(values, 0, rim_width, axis=direction + 1)
        below_live = (coords[direction] > 0).astype(jnp.float32)
        above_live = (coords[direction] < limits[direction] - 1).astype(jnp.float32)
        from_lower = from_behind(upper_face, "tile", strides[direction]) * below_live
        from_upper = from_behind(lower_face, "tile", -strides[direction]) * above_live
        values = jnp.concatenate([from_lower, values, from_upper], axis=direction + 1)
    return values


def local(residual, row_counts, recv_owner, recv_cell, conductivity, laplace, forward_field):
    tile_count = lax.axis_size("tile")
    tile_id = lax.axis_index("tile")
    layout = (
        (tile_id // (TY * TZ), tile_id // TZ % TY, tile_id % TZ),
        (tile_count // (TY * TZ), TY, TZ),
        (TY * TZ, TZ, 1),
    )
    residual_rows = residual[0]
    row_count = row_counts[0]
    recv_total = row_count.shape[0]
    row_total = residual_rows.shape[1]
    row_ends = jnp.cumsum(row_count)
    row_starts = row_ends - row_count
    positions = jnp.arange(row_total, dtype=jnp.int32)[None, :]
    member = ((positions >= row_starts[:, None]) & (positions < row_ends[:, None])).astype(
        jnp.float32
    )
    row_sums = lax.dot_general(
        residual_rows, member, (((1,), (1,)), ((), ())), precision=lax.Precision.HIGHEST
    )
    receiver_means = row_sums / row_count.astype(jnp.float32)[None, :]
    capacity = max(2, max(recv_total // 16, 2 * recv_total // tile_count))
    owner_tile = recv_owner[:, 0]
    owner_hits = (owner_tile[:, None] == jnp.arange(tile_count, dtype=jnp.int32)[None, :]).astype(
        jnp.int32
    )
    slot_rank = jnp.sum(jnp.cumsum(owner_hits, axis=0) * owner_hits, axis=1) - 1
    send_slot = owner_tile * capacity + slot_rank
    conduct_cells = conductivity[0]
    cell_total = conduct_cells.size
    send_values = (
        jnp.zeros((tile_count * capacity, 3), jnp.float32)
        .at[send_slot]
        .set(receiver_means.T)
        .reshape(tile_count, capacity, 3)
    )
    send_cells = (
        jnp.full((tile_count * capacity,), cell_total, jnp.int32)
        .at[send_slot]
        .set(recv_cell)
        .reshape(tile_count, capacity)
    )
    got_values, got_cells = (
        lax.all_to_all(send_values, "tile", split_axis=0, concat_axis=0, tiled=True),
        lax.all_to_all(send_cells, "tile", split_axis=0, concat_axis=0, tiled=True),
    )
    source = (
        jnp.zeros((3, cell_total), jnp.float32)
        .at[:, got_cells.reshape(-1)]
        .add(got_values.reshape(-1, 3).T, mode="drop")
        .reshape((3,) + conduct_cells.shape)
    )
    damping = laplace[0] * conduct_cells
    fixed_terms = jnp.concatenate([source, damping[None], jnp.ones_like(damping)[None]], axis=0)
    rim_width = 1

    def sweep_group(group_index, adjoint):
        padded = grow_rims(adjoint, rim_width, layout)
        padded = relax_sweep(padded, fixed_terms[:3], fixed_terms[3], fixed_terms[4])
        return padded

    adjoint = lax.fori_loop(0, SWEEPS // rim_width, sweep_group, jnp.zeros_like(source))
    partial_terms = (
        -laplace[0]
        * conduct_cells
        * jnp.sum(forward_field[0, 0].astype(jnp.float32) * adjoint, axis=0)
    )
    moved_rows = lax.all_to_all(
        partial_terms[None], "tile", split_axis=1, concat_axis=0, tiled=True
    )
    gradient = lax.psum_scatter(moved_rows, "freq", scatter_dimension=2, tiled=True)
    return gradient


def solution(mesh):
    placed = (
        P("freq", None, "tile"),
        P("tile", None),
        P("tile", None),
        P("tile"),
        P("tile", None, None, None),
        P("freq"),
        P("freq", "tile", None, None, None, None),
    )
    return jax.shard_map(
        local, mesh=mesh, in_specs=placed, out_specs=P(None, "tile", "freq", None), check_vma=False
    )
```

profile of v0, /device:TPU:1, one launch (start us, length us, event | category | flops | bytes accessed | tf_op | source)
XLA Modules:
  0.0 954.3 jit_solution(12431676112027179230)
XLA Ops:
  11.9 12.3 %all-to-all-start = ((s32[64,1,16]{2,1,0:T(1,128)}), s32[64,1,16]{2,1,0:T(1,128)S(1)}, u32[]{:S(2)}, u32[]{:S(2)}) async-start(s32[64,1,16]{2,1,0:T(1,128)} %bitcast.7), calls=%async_computation | async-start | bytes 65536 | tf_op jit(solution)/shard_map/all_to_all | solution.py:113
  33.6 10.3 %all-to-all-start.1 = ((f32[64,16,3]{1,2,0:T(4,128)}), f32[64,16,3]{1,2,0:T(4,128)S(1)}, u32[]{:S(2)}, u32[]{:S(2)}) async-start(f32[64,16,3]{1,2,0:T(4,128)} %copy.56), calls=%async_computation.1 | async-start | bytes 262144 | tf_op jit(solution)/shard_map/all_to_all | solution.py:112
  54.4 72.3 %scatter_custom_fusion.2 = f32[3,262144]{0,1:T(8,128)} fusion(s32[1024]{0:T(1024)S(1)} %get-tuple-element.221, f32[]{:T(128)} %constant.79.clone.1, f32[1024,3]{1,0:T(8,128)S(1)} %bitcast.72, s32[1024]{0:T(1024)S(1)} %broadcast_clamp_fusion), kind=kCustom, calls=%fused_computation.46 | custom fusion | flops 3072 | bytes 3145732 | tf_op jit(solution)/shard_map/scatter-add | solution.py:118
  126.6 70.6 %copy.59 = f32[3,64,32,128]{3,2,1,0:T(8,128)} copy(f32[3,64,32,128]{0,3,2,1:T(8,128)} %bitcast.15) | data formatting | bytes 6291456
  197.2 680.2 %while.13 = (s32[]{:T(128)}, f32[3,64,32,128]{3,2,1,0:T(8,128)}, pred[]{:T(512)}, pred[]{:T(512)}, pred[]{:T(512)}, /*index=5*/pred[]{:T(512)}, pred[]{:T(512)},...) while((s32[]{:T(128)}, f32[3,64,32,128]{3,2,1,0:T(8,128)}, ...), condition=%wide.region_9.10_spmd.clone, body=%wide.region_8.9_spmd.clone.sunk | while | flops 21863960 | bytes 101091864 | solution.py:130
  254.7 8.4 pad_maximum_fusion.10
  267.6 6.8 fusion.46
  284.3 7.4 collective-permute-start.1
  331.6 8.4 pad_maximum_fusion.10
  344.4 6.8 fusion.46
  361.1 17.1 %collective-permute-start.1 = (f32[3,1,32,128]{3,2,1,0:T(8,128)S(1)}, f32[3,1,32,128]{3,2,1,0:T(8,128)S(1)}, u32[]{:S(2)}, u32[]{:S(2)}) collective-permute-start(f32[3,1,32,128]{3,2,1,0:T(8,128)S(1)} %get-tuple-element.345), channel_id=1, source_target_pairs={{0,16},{1,17},{2,18},{3,19},{4,20},{5,21},{6,22},{7,23},{8,24},{9,... | collective-permute-start | bytes 147464 | tf_op jit(solution)/shard_map/while/body/eval_jaxpr/ppermute | solution.py:17
  418.2 8.4 pad_maximum_fusion.10
  447.8 17.0 %collective-permute-start.1 = (f32[3,1,32,128]{3,2,1,0:T(8,128)S(1)}, f32[3,1,32,128]{3,2,1,0:T(8,128)S(1)}, u32[]{:S(2)}, u32[]{:S(2)}) collective-permute-start(f32[3,1,32,128]{3,2,1,0:T(8,128)S(1)} %get-tuple-element.345), channel_id=1, source_target_pairs={{0,16},{1,17},{2,18},{3,19},{4,20},{5,21},{6,22},{7,23},{8,24},{9,... | collective-permute-start | bytes 147464 | tf_op jit(solution)/shard_map/while/body/eval_jaxpr/ppermute | solution.py:17
  504.9 8.4 pad_maximum_fusion.10
  534.4 17.0 %collective-permute-start.1 = (f32[3,1,32,128]{3,2,1,0:T(8,128)S(1)}, f32[3,1,32,128]{3,2,1,0:T(8,128)S(1)}, u32[]{:S(2)}, u32[]{:S(2)}) collective-permute-start(f32[3,1,32,128]{3,2,1,0:T(8,128)S(1)} %get-tuple-element.345), channel_id=1, source_target_pairs={{0,16},{1,17},{2,18},{3,19},{4,20},{5,21},{6,22},{7,23},{8,24},{9,... | collective-permute-start | bytes 147464 | tf_op jit(solution)/shard_map/while/body/eval_jaxpr/ppermute | solution.py:17
  591.5 8.4 pad_maximum_fusion.10
  621.1 17.0 %collective-permute-start.1 = (f32[3,1,32,128]{3,2,1,0:T(8,128)S(1)}, f32[3,1,32,128]{3,2,1,0:T(8,128)S(1)}, u32[]{:S(2)}, u32[]{:S(2)}) collective-permute-start(f32[3,1,32,128]{3,2,1,0:T(8,128)S(1)} %get-tuple-element.345), channel_id=1, source_target_pairs={{0,16},{1,17},{2,18},{3,19},{4,20},{5,21},{6,22},{7,23},{8,24},{9,... | collective-permute-start | bytes 147464 | tf_op jit(solution)/shard_map/while/body/eval_jaxpr/ppermute | solution.py:17
  678.1 8.4 pad_maximum_fusion.10
  707.7 17.0 %collective-permute-start.1 = (f32[3,1,32,128]{3,2,1,0:T(8,128)S(1)}, f32[3,1,32,128]{3,2,1,0:T(8,128)S(1)}, u32[]{:S(2)}, u32[]{:S(2)}) collective-permute-start(f32[3,1,32,128]{3,2,1,0:T(8,128)S(1)} %get-tuple-element.345), channel_id=1, source_target_pairs={{0,16},{1,17},{2,18},{3,19},{4,20},{5,21},{6,22},{7,23},{8,24},{9,... | collective-permute-start | bytes 147464 | tf_op jit(solution)/shard_map/while/body/eval_jaxpr/ppermute | solution.py:17
  764.8 8.4 pad_maximum_fusion.10
  794.3 17.0 %collective-permute-start.1 = (f32[3,1,32,128]{3,2,1,0:T(8,128)S(1)}, f32[3,1,32,128]{3,2,1,0:T(8,128)S(1)}, u32[]{:S(2)}, u32[]{:S(2)}) collective-permute-start(f32[3,1,32,128]{3,2,1,0:T(8,128)S(1)} %get-tuple-element.345), channel_id=1, source_target_pairs={{0,16},{1,17},{2,18},{3,19},{4,20},{5,21},{6,22},{7,23},{8,24},{9,... | collective-permute-start | bytes 147464 | tf_op jit(solution)/shard_map/while/body/eval_jaxpr/ppermute | solution.py:17
  851.4 8.4 pad_maximum_fusion.10
  880.7 47.6 %all_to_all.26 = f32[1,64,32,128]{3,2,0,1:T(8,128)} all-to-all(f32[1,64,32,128]{3,2,0,1:T(8,128)S(1)} %fusion.17), channel_id=1, replica_groups=mesh['freq'=2,'tile'=64] {'tile'}, dimensions={1} | all-to-all | bytes 2097152 | tf_op jit(solution)/shard_map/all_to_all | solution.py:136
  928.4 18.9 %reduce-scatter.2.cloned.1.call-done = f32[64,1,16,128]{3,2,0,1:T(8,128)} async-done(((f32[64,1,32,128]{3,2,0,1:T(8,128)}), f32[64,1,16,128]{3,2,0,1:T(8,128)}) %reduce-scatter.2.cloned.1.call-update) | async-done | bytes 524304 | tf_op jit(solution)/shard_map/reduce_scatter | solution.py:139
  (324 shorter events, 505.5 us)
Async XLA Ops:
  11.9 21.7 %all-to-all-start = ((s32[64,1,16]{2,1,0:T(1,128)}), s32[64,1,16]{2,1,0:T(1,128)S(1)}, u32[]{:S(2)}, u32[]{:S(2)}) async-start(s32[64,1,16]{2,1,0:T(1,128)} %bitcast.7), calls=%async_computation | async-start | bytes 65536 | tf_op jit(solution)/shard_map/all_to_all | solution.py:113
  33.6 20.4 %all-to-all-start.1 = ((f32[64,16,3]{1,2,0:T(4,128)}), f32[64,16,3]{1,2,0:T(4,128)S(1)}, u32[]{:S(2)}, u32[]{:S(2)}) async-start(f32[64,16,3]{1,2,0:T(4,128)} %copy.56), calls=%async_computation.1 | async-start | bytes 262144 | tf_op jit(solution)/shard_map/all_to_all | solution.py:112
  43.9 903.4 %reduce-scatter.2.cloned.1.call-start = ((), (), s32[]{:S(2)}) async-start(), calls=%async_computation.4 | async-start | bytes 1572864 | tf_op jit(solution)/shard_map/reduce_scatter | solution.py:139
  233.7 12.9 %collective-permute-start.4 = (f32[3,66,34,1]{1,3,2,0:T(1,128)S(1)}, f32[3,66,34,1]{1,3,2,0:T(1,128)}, u32[]{:S(2)}, u32[]{:S(2)}) collective-permute-start(f32[3,66,34,1]{1,3,2,0:T(1,128)S(1)} %copy.78), channel_id=1, source_target_pairs={{1,0},{2,1},{3,2},{4,3},{5,4},{6,5},{7,6},{8,7},{9,8},{10,9},{11,1... | collective-permute-start | bytes 80792 | tf_op jit(solution)/shard_map/while/body/eval_jaxpr/ppermute | solution.py:17
  283.0 8.7 collective-permute-start
  310.3 13.1 %collective-permute-start.4 = (f32[3,66,34,1]{1,3,2,0:T(1,128)S(1)}, f32[3,66,34,1]{1,3,2,0:T(1,128)}, u32[]{:S(2)}, u32[]{:S(2)}) collective-permute-start(f32[3,66,34,1]{1,3,2,0:T(1,128)S(1)} %copy.78), channel_id=1, source_target_pairs={{1,0},{2,1},{3,2},{4,3},{5,4},{6,5},{7,6},{8,7},{9,8},{10,9},{11,1... | collective-permute-start | bytes 80792 | tf_op jit(solution)/shard_map/while/body/eval_jaxpr/ppermute | solution.py:17
  359.8 18.4 %collective-permute-start = (f32[3,1,32,128]{3,2,1,0:T(8,128)S(1)}, f32[3,1,32,128]{3,2,1,0:T(8,128)S(1)}, u32[]{:S(2)}, u32[]{:S(2)}) collective-permute-start(f32[3,1,32,128]{3,2,1,0:T(8,128)S(1)} %get-tuple-element.344), channel_id=1, source_target_pairs={{16,0},{17,1},{18,2},{19,3},{20,4},{21,5},{22,6},{23,7},{24,8},{25... | collective-permute-start | bytes 147464 | tf_op jit(solution)/shard_map/while/body/eval_jaxpr/ppermute | solution.py:17
  361.1 18.2 %collective-permute-start.1 = (f32[3,1,32,128]{3,2,1,0:T(8,128)S(1)}, f32[3,1,32,128]{3,2,1,0:T(8,128)S(1)}, u32[]{:S(2)}, u32[]{:S(2)}) collective-permute-start(f32[3,1,32,128]{3,2,1,0:T(8,128)S(1)} %get-tuple-element.345), channel_id=1, source_target_pairs={{0,16},{1,17},{2,18},{3,19},{4,20},{5,21},{6,22},{7,23},{8,24},{9,... | collective-permute-start | bytes 147464 | tf_op jit(solution)/shard_map/while/body/eval_jaxpr/ppermute | solution.py:17
  396.6 13.5 %collective-permute-start.4 = (f32[3,66,34,1]{1,3,2,0:T(1,128)S(1)}, f32[3,66,34,1]{1,3,2,0:T(1,128)}, u32[]{:S(2)}, u32[]{:S(2)}) collective-permute-start(f32[3,66,34,1]{1,3,2,0:T(1,128)S(1)} %copy.78), channel_id=1, source_target_pairs={{1,0},{2,1},{3,2},{4,3},{5,4},{6,5},{7,6},{8,7},{9,8},{10,9},{11,1... | collective-permute-start | bytes 80792 | tf_op jit(solution)/shard_map/while/body/eval_jaxpr/ppermute | solution.py:17
  446.5 18.3 %collective-permute-start = (f32[3,1,32,128]{3,2,1,0:T(8,128)S(1)}, f32[3,1,32,128]{3,2,1,0:T(8,128)S(1)}, u32[]{:S(2)}, u32[]{:S(2)}) collective-permute-start(f32[3,1,32,128]{3,2,1,0:T(8,128)S(1)} %get-tuple-element.344), channel_id=1, source_target_pairs={{16,0},{17,1},{18,2},{19,3},{20,4},{21,5},{22,6},{23,7},{24,8},{25... | collective-permute-start | bytes 147464 | tf_op jit(solution)/shard_map/while/body/eval_jaxpr/ppermute | solution.py:17
  447.8 18.2 %collective-permute-start.1 = (f32[3,1,32,128]{3,2,1,0:T(8,128)S(1)}, f32[3,1,32,128]{3,2,1,0:T(8,128)S(1)}, u32[]{:S(2)}, u32[]{:S(2)}) collective-permute-start(f32[3,1,32,128]{3,2,1,0:T(8,128)S(1)} %get-tuple-element.345), channel_id=1, source_target_pairs={{0,16},{1,17},{2,18},{3,19},{4,20},{5,21},{6,22},{7,23},{8,24},{9,... | collective-permute-start | bytes 147464 | tf_op jit(solution)/shard_map/while/body/eval_jaxpr/ppermute | solution.py:17
  483.3 13.5 %collective-permute-start.4 = (f32[3,66,34,1]{1,3,2,0:T(1,128)S(1)}, f32[3,66,34,1]{1,3,2,0:T(1,128)}, u32[]{:S(2)}, u32[]{:S(2)}) collective-permute-start(f32[3,66,34,1]{1,3,2,0:T(1,128)S(1)} %copy.78), channel_id=1, source_target_pairs={{1,0},{2,1},{3,2},{4,3},{5,4},{6,5},{7,6},{8,7},{9,8},{10,9},{11,1... | collective-permute-start | bytes 80792 | tf_op jit(solution)/shard_map/while/body/eval_jaxpr/ppermute | solution.py:17
  533.1 18.3 %collective-permute-start = (f32[3,1,32,128]{3,2,1,0:T(8,128)S(1)}, f32[3,1,32,128]{3,2,1,0:T(8,128)S(1)}, u32[]{:S(2)}, u32[]{:S(2)}) collective-permute-start(f32[3,1,32,128]{3,2,1,0:T(8,128)S(1)} %get-tuple-element.344), channel_id=1, source_target_pairs={{16,0},{17,1},{18,2},{19,3},{20,4},{21,5},{22,6},{23,7},{24,8},{25... | collective-permute-start | bytes 147464 | tf_op jit(solution)/shard_map/while/body/eval_jaxpr/ppermute | solution.py:17
  534.4 18.2 %collective-permute-start.1 = (f32[3,1,32,128]{3,2,1,0:T(8,128)S(1)}, f32[3,1,32,128]{3,2,1,0:T(8,128)S(1)}, u32[]{:S(2)}, u32[]{:S(2)}) collective-permute-start(f32[3,1,32,128]{3,2,1,0:T(8,128)S(1)} %get-tuple-element.345), channel_id=1, source_target_pairs={{0,16},{1,17},{2,18},{3,19},{4,20},{5,21},{6,22},{7,23},{8,24},{9,... | collective-permute-start | bytes 147464 | tf_op jit(solution)/shard_map/while/body/eval_jaxpr/ppermute | solution.py:17
  569.9 13.5 %collective-permute-start.4 = (f32[3,66,34,1]{1,3,2,0:T(1,128)S(1)}, f32[3,66,34,1]{1,3,2,0:T(1,128)}, u32[]{:S(2)}, u32[]{:S(2)}) collective-permute-start(f32[3,66,34,1]{1,3,2,0:T(1,128)S(1)} %copy.78), channel_id=1, source_target_pairs={{1,0},{2,1},{3,2},{4,3},{5,4},{6,5},{7,6},{8,7},{9,8},{10,9},{11,1... | collective-permute-start | bytes 80792 | tf_op jit(solution)/shard_map/while/body/eval_jaxpr/ppermute | solution.py:17
  619.8 18.3 %collective-permute-start = (f32[3,1,32,128]{3,2,1,0:T(8,128)S(1)}, f32[3,1,32,128]{3,2,1,0:T(8,128)S(1)}, u32[]{:S(2)}, u32[]{:S(2)}) collective-permute-start(f32[3,1,32,128]{3,2,1,0:T(8,128)S(1)} %get-tuple-element.344), channel_id=1, source_target_pairs={{16,0},{17,1},{18,2},{19,3},{20,4},{21,5},{22,6},{23,7},{24,8},{25... | collective-permute-start | bytes 147464 | tf_op jit(solution)/shard_map/while/body/eval_jaxpr/ppermute | solution.py:17
  621.1 18.2 %collective-permute-start.1 = (f32[3,1,32,128]{3,2,1,0:T(8,128)S(1)}, f32[3,1,32,128]{3,2,1,0:T(8,128)S(1)}, u32[]{:S(2)}, u32[]{:S(2)}) collective-permute-start(f32[3,1,32,128]{3,2,1,0:T(8,128)S(1)} %get-tuple-element.345), channel_id=1, source_target_pairs={{0,16},{1,17},{2,18},{3,19},{4,20},{5,21},{6,22},{7,23},{8,24},{9,... | collective-permute-start | bytes 147464 | tf_op jit(solution)/shard_map/while/body/eval_jaxpr/ppermute | solution.py:17
  656.5 13.5 %collective-permute-start.4 = (f32[3,66,34,1]{1,3,2,0:T(1,128)S(1)}, f32[3,66,34,1]{1,3,2,0:T(1,128)}, u32[]{:S(2)}, u32[]{:S(2)}) collective-permute-start(f32[3,66,34,1]{1,3,2,0:T(1,128)S(1)} %copy.78), channel_id=1, source_target_pairs={{1,0},{2,1},{3,2},{4,3},{5,4},{6,5},{7,6},{8,7},{9,8},{10,9},{11,1... | collective-permute-start | bytes 80792 | tf_op jit(solution)/shard_map/while/body/eval_jaxpr/ppermute | solution.py:17
  706.4 18.3 %collective-permute-start = (f32[3,1,32,128]{3,2,1,0:T(8,128)S(1)}, f32[3,1,32,128]{3,2,1,0:T(8,128)S(1)}, u32[]{:S(2)}, u32[]{:S(2)}) collective-permute-start(f32[3,1,32,128]{3,2,1,0:T(8,128)S(1)} %get-tuple-element.344), channel_id=1, source_target_pairs={{16,0},{17,1},{18,2},{19,3},{20,4},{21,5},{22,6},{23,7},{24,8},{25... | collective-permute-start | bytes 147464 | tf_op jit(solution)/shard_map/while/body/eval_jaxpr/ppermute | solution.py:17
  707.7 18.2 %collective-permute-start.1 = (f32[3,1,32,128]{3,2,1,0:T(8,128)S(1)}, f32[3,1,32,128]{3,2,1,0:T(8,128)S(1)}, u32[]{:S(2)}, u32[]{:S(2)}) collective-permute-start(f32[3,1,32,128]{3,2,1,0:T(8,128)S(1)} %get-tuple-element.345), channel_id=1, source_target_pairs={{0,16},{1,17},{2,18},{3,19},{4,20},{5,21},{6,22},{7,23},{8,24},{9,... | collective-permute-start | bytes 147464 | tf_op jit(solution)/shard_map/while/body/eval_jaxpr/ppermute | solution.py:17
  743.2 13.5 %collective-permute-start.4 = (f32[3,66,34,1]{1,3,2,0:T(1,128)S(1)}, f32[3,66,34,1]{1,3,2,0:T(1,128)}, u32[]{:S(2)}, u32[]{:S(2)}) collective-permute-start(f32[3,66,34,1]{1,3,2,0:T(1,128)S(1)} %copy.78), channel_id=1, source_target_pairs={{1,0},{2,1},{3,2},{4,3},{5,4},{6,5},{7,6},{8,7},{9,8},{10,9},{11,1... | collective-permute-start | bytes 80792 | tf_op jit(solution)/shard_map/while/body/eval_jaxpr/ppermute | solution.py:17
  793.0 18.3 %collective-permute-start = (f32[3,1,32,128]{3,2,1,0:T(8,128)S(1)}, f32[3,1,32,128]{3,2,1,0:T(8,128)S(1)}, u32[]{:S(2)}, u32[]{:S(2)}) collective-permute-start(f32[3,1,32,128]{3,2,1,0:T(8,128)S(1)} %get-tuple-element.344), channel_id=1, source_target_pairs={{16,0},{17,1},{18,2},{19,3},{20,4},{21,5},{22,6},{23,7},{24,8},{25... | collective-permute-start | bytes 147464 | tf_op jit(solution)/shard_map/while/body/eval_jaxpr/ppermute | solution.py:17
  794.3 18.2 %collective-permute-start.1 = (f32[3,1,32,128]{3,2,1,0:T(8,128)S(1)}, f32[3,1,32,128]{3,2,1,0:T(8,128)S(1)}, u32[]{:S(2)}, u32[]{:S(2)}) collective-permute-start(f32[3,1,32,128]{3,2,1,0:T(8,128)S(1)} %get-tuple-element.345), channel_id=1, source_target_pairs={{0,16},{1,17},{2,18},{3,19},{4,20},{5,21},{6,22},{7,23},{8,24},{9,... | collective-permute-start | bytes 147464 | tf_op jit(solution)/shard_map/while/body/eval_jaxpr/ppermute | solution.py:17
  829.8 13.5 %collective-permute-start.4 = (f32[3,66,34,1]{1,3,2,0:T(1,128)S(1)}, f32[3,66,34,1]{1,3,2,0:T(1,128)}, u32[]{:S(2)}, u32[]{:S(2)}) collective-permute-start(f32[3,66,34,1]{1,3,2,0:T(1,128)S(1)} %copy.78), channel_id=1, source_target_pairs={{1,0},{2,1},{3,2},{4,3},{5,4},{6,5},{7,6},{8,7},{9,8},{10,9},{11,1... | collective-permute-start | bytes 80792 | tf_op jit(solution)/shard_map/while/body/eval_jaxpr/ppermute | solution.py:17
  (47 other events, 323.8 us)
Sparse Core Ops, SparseCore 0:
  928.5 18.7 reduce-scatter.1
where the time goes:
time: 960 us; the launch traced here: 954 us
  other arithmetic  333 us (35%)
  starting transfers between devices  262 us (27%)
  local copies, waits for them, and re-layouts  240 us (25%)
  blocking collectives  47.6 us (5%)
  waiting for transfers between devices  45.3 us (5%)
  between operations  14.4 us (2%)
  loops' own time  12.2 us (1%)
    ppermute x48, starting transfers between devices, from_behind(): return lax.ppermute(array, axis, pairs)  239 us
    scatter-add x3, other arithmetic, local(): source = jnp.zeros((3, cell_total), jnp.float32).at[:, got_cells.reshape(...  76 us
    concatenate x16, other arithmetic, grow_rims(): jnp.concatenate([from_lower, values, from_upper], axis=direction + 1)  72.1 us
    unnamed x9, local copies, waits for them, and re-layouts  70.6 us
    slice x24, local copies, waits for them, and re-layouts, grow_rims(): lax.slice_in_dim(values, extent - rim_width, extent, axis=direction + 1)  63.8 us
    another operation x8, other arithmetic, curl_curl(): jnp.stack([backward_step(swirl_z, 1) - backward_step(swirl_y, 2), backwar...  54.5 us
    all_to_all x1, blocking collectives, local(): lax.all_to_all(partial_terms[None], 'tile', split_axis=1, concat_axis=0,...  47.6 us
    add x8, other arithmetic, relax_sweep(): centre + RELAXATION * (source - curl_curl(padded) - damping * centre) / (...  36.8 us
  transfers between devices with their start and end apart: 51, of which 27 were waited for; matrix products, arithmetic and copies ran while one was open for 10% of the time, Pallas kernels for 0%

commit v1 on v0

v1 whole, which is shorter than its diff:
```python
import functools

import jax
import jax.numpy as jnp
from jax import lax
from jax.experimental import pallas as pl
from jax.experimental.pallas import tpu as pltpu
from jax.sharding import PartitionSpec as P

F32 = jnp.float32
BF16 = jnp.bfloat16
I32 = jnp.int32
MESH = pl.DeviceIdType.MESH

TX, TY, TZ = 4, 4, 4
TILES = 64
CX, CY, CZ = 64, 32, 128
RIM = 7

YR = 56
B0 = 81
RUN = 26
SEG = 42
PLANES = 112
OWN = 8


def iota(shape, dim):
    return lax.broadcasted_iota(I32, shape, dim)


def vmem():
    return pl.BlockSpec(memory_space=pltpu.VMEM)


def hbm():
    return pl.BlockSpec(memory_space=pl.ANY)


def place(t):
    return t // (TY * TZ), (t // TZ) % TY, t % TZ


def three(value):
    hi = value.astype(BF16)
    rest = value - hi.astype(F32)
    mid = rest.astype(BF16)
    low = (rest - mid.astype(F32)).astype(BF16)
    return hi, mid, low


def pack_own(read, s, rows, moves):
    lane = iota((rows, 128), 1)
    total = jnp.zeros((rows, 128), F32)
    for g in range(3):
        plane = read(1 + RUN * g + s)
        for begin, end, shift in moves:
            moved = pltpu.roll(plane, (SEG * g + shift) % 128, 1)
            total = jnp.where((lane >= SEG * g + begin) & (lane < SEG * g + end), moved, total)
    return total


def gather_kernel(res_ref, cnt_ref, idx_ref, lap_ref, cond_ref, list_ref, coef_ref,
                  cext, pack, low, high, sends, recvs, zsend, zrecv, gsend, grecv, lsem):
    f, t = lax.axis_index("freq"), lax.axis_index("tile")
    tx, ty, tz = place(t)
    barrier = pltpu.get_barrier_semaphore()

    def greet(i, c):
        pl.semaphore_signal(barrier, inc=1, device_id=(f, (t + i) % TILES), device_id_type=MESH)
        return c

    lax.fori_loop(1, TILES, greet, 0)
    own = pltpu.make_async_copy(cond_ref, cext.at[pl.ds(OWN, CX), pl.ds(8, CY)], lsem)
    own.start()

    counts = cnt_ref[...].astype(F32)
    upto = (iota((256, 256), 0) <= iota((256, 256), 1)).astype(F32)
    ends = jnp.dot(jnp.broadcast_to(counts, (8, 256)).astype(BF16), upto.astype(BF16), preferred_element_type=F32)[0:1]
    starts = ends - counts
    at = iota((1024, 256), 0).astype(F32)
    member = ((at >= starts) & (at < ends)).astype(F32).astype(BF16)
    sums = jnp.zeros((3, 256), F32)
    for part in three(res_ref[0]):
        sums = sums + jnp.dot(part, member, preferred_element_type=F32)
    means = sums / counts
    both = jnp.concatenate([means, idx_ref[...]], axis=0)
    list_ref[t] = jnp.concatenate([both[:, :128], both[:, 128:]], axis=0)

    pl.semaphore_wait(barrier, TILES - 1)

    def share(i, c):
        pltpu.make_async_remote_copy(list_ref.at[t], list_ref.at[t], gsend, grecv,
                                     device_id=(f, (t + i) % TILES), device_id_type=MESH).start()
        return c

    lax.fori_loop(1, TILES, share, 0)

    spans = {1: (CX - 7, 1, 7), -1: (0, 72, 7), 0: (0, 8, CX)}
    rows = {1: (CY - 8, 0, 8), -1: (0, 40, 8), 0: (0, 8, CY)}
    ways = [(dx, dy) for dx in (-1, 0, 1) for dy in (-1, 0, 1) if (dx, dy) != (0, 0)]

    def inside(dx, dy):
        x, y = tx + dx, ty + dy
        return (x >= 0) & (x < TX) & (y >= 0) & (y < TY)

    def halo(n):
        dx, dy = ways[n]
        xs, xd, xn = spans[dx]
        ys, yd, yn = rows[dy]
        return pltpu.make_async_remote_copy(
            cond_ref.at[pl.ds(xs, xn), pl.ds(ys, yn)], cext.at[pl.ds(xd, xn), pl.ds(yd, yn)],
            sends.at[n], recvs.at[n], device_id=(f, t + dx * TY * TZ + dy * TZ), device_id_type=MESH)

    for n, (dx, dy) in enumerate(ways):
        @pl.when(inside(dx, dy))
        def _(n=n):
            halo(n).start()
    own.wait()
    for n, (dx, dy) in enumerate(ways):
        @pl.when(inside(-dx, -dy))
        def _(n=n):
            halo(n).wait_recv()

    def read(i):
        return cext[i]

    def fill(s, c):
        pack[s] = pack_own(read, s, 48, ((0, 7, -121), (35, 42, 35)))
        return c

    lax.fori_loop(0, RUN, fill, 0)

    def rim(up):
        return pltpu.make_async_remote_copy(
            pack, low if up else high, zsend.at[up], zrecv.at[up],
            device_id=(f, t + (1 if up else -1)), device_id_type=MESH)

    @pl.when(tz < TZ - 1)
    def _():
        rim(1).start()

    @pl.when(tz > 0)
    def _():
        rim(0).start()

    lap = lap_ref[0]
    yrow = iota((48, 128), 0) - 8
    yin = (yrow + ty * CY >= 0) & (yrow + ty * CY < TY * CY)

    def fill_a(i, c):
        x = i - 8 + tx * CX
        good = yin & (x >= 0) & (x < TX * CX)
        coef_ref[i, pl.ds(0, 48), :] = jnp.where(good, 1.0 / (4.0 + lap * cext[i]), 0.0)
        return c

    lax.fori_loop(0, 80, fill_a, 0)

    @pl.when(tz > 0)
    def _():
        rim(1).wait_recv()

    @pl.when(tz < TZ - 1)
    def _():
        rim(0).wait_recv()

    lane = iota((48, 128), 1)
    run = (lane >= SEG).astype(I32) + (lane >= 2 * SEG).astype(I32)
    seg = lane - run * SEG
    z = jnp.where(seg < 21, seg - 7, seg + 93) + tz * CZ
    zin = (z >= 0) & (z < TZ * CZ) & (lane < 3 * SEG)

    def fill_b(s, c):
        value = pack_own(read, s, 48, ((7, 21, 7), (21, 35, -93)))
        value = jnp.where(seg < 7, low[s], jnp.where(seg >= 35, high[s], value))
        x = RUN * run + s - 7 + tx * CX
        good = yin & zin & (x >= 0) & (x < TX * CX)
        coef_ref[B0 + s, pl.ds(0, 48), :] = jnp.where(good, 1.0 / (4.0 + lap * value), 0.0)
        return c

    lax.fori_loop(0, RUN, fill_b, 0)

    for n, (dx, dy) in enumerate(ways):
        @pl.when(inside(dx, dy))
        def _(n=n):
            halo(n).wait_send()

    @pl.when(tz < TZ - 1)
    def _():
        rim(1).wait_send()

    @pl.when(tz > 0)
    def _():
        rim(0).wait_send()

    everyone = list_ref.at[pl.ds(0, TILES - 1)]
    pltpu.make_async_copy(everyone, everyone, gsend).wait()
    pltpu.make_async_copy(everyone, everyone, grecv).wait()


def stencil(src, dst, base, coef, hx_ref, hy_ref, hz_ref, lo, hi, y0, nk, nh, scale):
    rk, rh, h0 = 8 * nk, 8 * nh, y0 - 1
    hr, hy_rows, kr, kl = pl.ds(h0, rh), pl.ds(y0, rh), pl.ds(y0, rk), pl.ds(h0, rk)

    def swirl(x):
        vx, vy, vz = src[0, x, hr, :], src[1, x, hr, :], src[2, x, hr, :]
        vyz, vxz = pltpu.roll(vy, 127, 1), pltpu.roll(vx, 127, 1)
        hx_ref[x, hr, :] = (src[2, x, hy_rows, :] - vz) - (vyz - vy)
        hy_ref[x, hr, :] = (vxz - vx) - (src[2, x + 1, hr, :] - vz)
        hz_ref[x, hr, :] = (src[1, x + 1, hr, :] - vy) - (src[0, x, hy_rows, :] - vx)

    def relax(x):
        hx, hy, hz = hx_ref[x, kr, :], hy_ref[x, kr, :], hz_ref[x, kr, :]
        kx = (hz - hz_ref[x, kl, :]) - (hy - pltpu.roll(hy, 1, 1))
        ky = (hx - pltpu.roll(hx, 1, 1)) - (hz - hz_ref[x - 1, kr, :])
        kz = (hy - hy_ref[x - 1, kr, :]) - (hx - hx_ref[x, kl, :])
        c = coef[x, kr, :]
        keep = 1.0 + 4.0 * c
        for i, k in enumerate((kx, ky, kz)):
            new = keep * src[i, x, kr, :] - c * k
            if base is not None:
                new = base[i, x, kr, :] + scale * new
            dst[i, x, kr, :] = new

    swirl(lo - 1)
    swirl(lo)

    def body(x, c):
        relax(x)
        swirl(x + 1)
        return c

    lax.fori_loop(lo, hi, body, 0)


def relax_kernel(list_ref, lap_ref, coef_hbm, cond_hbm, field_hbm, out_ref,
                 u, p, q, hx_ref, hy_ref, hz_ref, coef, cond, field, spots, vals, val_s, cnt_s,
                 sems, cnt_v):
    t = lax.axis_index("tile")
    tx, ty, tz = place(t)
    loads = [pltpu.make_async_copy(a, b, sems.at[n])
             for n, (a, b) in enumerate(((coef_hbm, coef), (cond_hbm, cond), (field_hbm, field)))]
    for copy in loads:
        copy.start()

    flat = u.reshape(3, PLANES * YR, 128)

    def clear(i, c):
        for k in range(3):
            u[k, i] = jnp.zeros((YR, 128), F32)
        return c

    lax.fori_loop(0, PLANES, clear, 0)

    before = (iota((128, 128), 0) < iota((128, 128), 1)).astype(F32).astype(BF16)
    for half in range(2):
        code = list_ref[:, 4 * half + 3, :].astype(I32)
        x = (code >> 16) - tx * CX + RIM
        y = ((code >> 9) & 127) - ty * CY + RIM
        z = (code & 511) - tz * CZ
        ok = (x >= 0) & (x < CX + 2 * RIM) & (y >= 0) & (y < CY + 2 * RIM) & (z >= -RIM) & (z < CZ + RIM)
        run = (x >= RUN).astype(I32) + (x >= 2 * RUN).astype(I32)
        in_a = (z >= 0) & (z < CZ)
        plane = jnp.where(in_a, x + 1, x - RUN * run + B0)
        lane = jnp.where(in_a, z, SEG * run + jnp.where(z < 0, z + 7, z - 93))
        spot = (plane * YR + y + 1) * 128 + lane
        flag = ok.astype(F32)
        rank = jnp.dot(flag.astype(BF16), before, preferred_element_type=F32)
        spots[half, 0] = jnp.where(ok, spot, 0).astype(F32)
        spots[half, 1] = jnp.where(ok, rank, -1.0)
        cnt_v[half] = jnp.broadcast_to(jnp.sum(flag, axis=1, keepdims=True), (TILES, 128)).astype(I32)
    place_k = iota((128, 128), 0).astype(F32)

    def squeeze(b, c):
        for half in range(2):
            values = list_ref[b, pl.ds(4 * half, 3), :]
            both = jnp.concatenate([values, spots[half, 0, pl.ds(b, 1), :]], axis=0)
            pick = (place_k == spots[half, 1, pl.ds(b, 1), :]).astype(F32).astype(BF16)
            got = jnp.zeros((4, 128), F32)
            for part in three(both):
                got = got + lax.dot_general(part, pick, (((1,), (1,)), ((), ())), preferred_element_type=F32)
            vals[2 * b + half] = jnp.concatenate([got, jnp.zeros((4, 128), F32)], axis=0)
        return c

    lax.fori_loop(0, TILES, squeeze, 0)
    to_s = [pltpu.make_async_copy(vals, val_s, sems.at[3]), pltpu.make_async_copy(cnt_v, cnt_s, sems.at[4])]
    for copy in to_s:
        copy.start()
    for copy in to_s:
        copy.wait()
    lane_id = iota((1, 128), 1)

    def drop(b, c):
        def one(k, c2):
            spot = val_s[b, 3, k].astype(I32)
            row, lane = spot >> 7, spot & 127
            here = lane_id == lane
            for i in range(3):
                flat[i, pl.ds(row, 1), :] += jnp.where(here, val_s[b, i, k], 0.0)
            return c2

        lax.fori_loop(0, cnt_s[b % 2, b // 2, 0], one, 0)
        return c

    lax.fori_loop(0, 2 * TILES, drop, 0)
    loads[0].wait()

    def scale_b(s, c):
        for i in range(3):
            value = pack_own(lambda k: u[i, k], s, YR, ((7, 21, 7), (21, 35, -93))) + u[i, B0 + s]
            u[i, B0 + s] = 0.5 * coef[B0 + s] * value
        return c

    lax.fori_loop(0, RUN, scale_b, 0)

    def scale_a(k, c):
        for i in range(3):
            u[i, k] = 0.5 * coef[k] * u[i, k]
        return c

    lax.fori_loop(0, 80, scale_a, 0)

    plan = [(u, p, u, 0.5), (p, q, None, 1.0), (q, u, p, 0.25), (u, p, None, 1.0), (p, q, None, 1.0),
            (q, p, None, 1.0), (p, q, u, 0.0625)]
    for n, (src, dst, base, scale) in enumerate(plan):
        e = RIM - 1 - n
        nk, nh = -(-(CY + 2 * e) // 8), -(-(CY + 1 + 2 * e) // 8)
        for i in range(3):
            src[i, B0 - 1] = pltpu.roll(src[i, B0 + RUN - 1], SEG, 1)
            src[i, B0 + RUN] = pltpu.roll(src[i, B0], 128 - SEG, 1)
        stencil(src, dst, base, coef, hx_ref, hy_ref, hz_ref, B0, B0 + RUN, 8 - e, nk, nh, scale)
        stencil(src, dst, base, coef, hx_ref, hy_ref, hz_ref, OWN - e, OWN + CX + e, 8 - e, nk, nh, scale)

    loads[1].wait()
    loads[2].wait()
    lane = iota((CY, 128), 1)
    own_y = pl.ds(8, CY)
    lap = lap_ref[0]
    for g, (begin, end) in enumerate(((0, 19), (19, 45), (45, 64))):
        def combine(x, c, g=g):
            total = jnp.zeros((CY, 128), F32)
            for i in range(3):
                rims = q[i, B0 + x + RIM - RUN * g, own_y, :]
                value = jnp.where(lane < RIM, pltpu.roll(rims, (-(SEG * g + 7)) % 128, 1),
                                  jnp.where(lane >= CZ - RIM, pltpu.roll(rims, (93 - SEG * g) % 128, 1),
                                            q[i, OWN + x, own_y, :]))
                total = total + field[i, x].astype(F32) * value
            out_ref[x] = -lap * cond[x] * total
            return c

        lax.fori_loop(begin, end, combine, 0)


def spread_kernel(part_ref, out_ref, send, recv, lsem):
    f, t = lax.axis_index("freq"), lax.axis_index("tile")
    me = f * TILES + t
    barrier = pltpu.get_barrier_semaphore()

    def peer(i):
        d = (me + i) % (2 * TILES)
        return d // TILES, d % TILES

    def greet(i, c):
        pl.semaphore_signal(barrier, inc=1, device_id=peer(i), device_id_type=MESH)
        return c

    lax.fori_loop(1, 2 * TILES, greet, 0)
    mine = pltpu.make_async_copy(part_ref.at[t, pl.ds(f * 16, 16)], out_ref.at[me], lsem)
    mine.start()
    pl.semaphore_wait(barrier, 2 * TILES - 1)

    def share(i, c):
        df, dt = peer(i)
        pltpu.make_async_remote_copy(part_ref.at[dt, pl.ds(df * 16, 16)], out_ref.at[me], send, recv,
                                     device_id=(df, dt), device_id_type=MESH).start()
        return c

    lax.fori_loop(1, 2 * TILES, share, 0)
    mine.wait()
    others = out_ref.at[pl.ds(0, 2 * TILES - 1)]
    for sem in (send, recv):
        pltpu.make_async_copy(others, others, sem).wait()


def local(residual, row_counts, recv_owner, recv_cell, conductivity, laplace, forward_field):
    owner = recv_owner[:, 0]
    gx = (owner // (TY * TZ)) * CX + recv_cell // (CY * CZ)
    gy = (owner // TZ % TY) * CY + recv_cell // CZ % CY
    gz = (owner % TZ) * CZ + recv_cell % CZ
    codes = ((gx * (TY * CY) + gy) * (TZ * CZ) + gz).astype(F32)[None]
    smem = pl.BlockSpec(memory_space=pltpu.SMEM)
    cond = conductivity[0]
    lists, coef = pl.pallas_call(
        gather_kernel,
        name="gather_lists",
        out_shape=(jax.ShapeDtypeStruct((TILES, 8, 128), F32), jax.ShapeDtypeStruct((PLANES, YR, 128), F32)),
        in_specs=[vmem(), vmem(), vmem(), smem, hbm()],
        out_specs=(vmem(), vmem()),
        scratch_shapes=[
            pltpu.VMEM((80, 48, 128), F32),
            pltpu.VMEM((RUN, 48, 128), F32),
            pltpu.VMEM((RUN, 48, 128), F32),
            pltpu.VMEM((RUN, 48, 128), F32),
            pltpu.SemaphoreType.DMA((8,)),
            pltpu.SemaphoreType.DMA((8,)),
            pltpu.SemaphoreType.DMA((2,)),
            pltpu.SemaphoreType.DMA((2,)),
            pltpu.SemaphoreType.DMA,
            pltpu.SemaphoreType.DMA,
            pltpu.SemaphoreType.DMA,
        ],
        compiler_params=pltpu.CompilerParams(collective_id=0, has_side_effects=True, vmem_limit_bytes=32 * 2**20),
    )(residual, row_counts, codes, laplace, cond)
    partial = pl.pallas_call(
        relax_kernel,
        name="relax_tile",
        out_shape=jax.ShapeDtypeStruct((CX, CY, CZ), F32),
        in_specs=[vmem(), smem, hbm(), hbm(), hbm()],
        out_specs=vmem(),
        scratch_shapes=[pltpu.VMEM((3, PLANES, YR, 128), F32)] * 3
        + [pltpu.VMEM((PLANES, YR, 128), F32)] * 4
        + [
            pltpu.VMEM((CX, CY, CZ), F32),
            pltpu.VMEM((3, CX, CY, CZ), BF16),
            pltpu.VMEM((2, 2, TILES, 128), F32),
            pltpu.VMEM((2 * TILES, 8, 128), F32),
            pltpu.SMEM((2 * TILES, 8, 128), F32),
            pltpu.SMEM((2, TILES, 128), I32),
            pltpu.SemaphoreType.DMA((5,)),
            pltpu.VMEM((2, TILES, 128), I32),
        ],
        compiler_params=pltpu.CompilerParams(vmem_limit_bytes=58 * 2**20),
    )(lists, laplace, coef, cond, forward_field[0, 0])
    both = pl.pallas_call(
        spread_kernel,
        name="spread_rows",
        out_shape=jax.ShapeDtypeStruct((2 * TILES, 16, CZ), F32),
        in_specs=[hbm()],
        out_specs=hbm(),
        scratch_shapes=[pltpu.SemaphoreType.DMA] * 3,
        compiler_params=pltpu.CompilerParams(collective_id=1, has_side_effects=True),
    )(partial)
    return (both[:TILES] + both[TILES:])[:, None]


def solution(mesh):
    placed = (
        P("freq", None, "tile"),
        P("tile", None),
        P("tile", None),
        P("tile"),
        P("tile", None, None, None),
        P("freq"),
        P("freq", "tile", None, None, None, None),
    )
    return jax.shard_map(
        local, mesh=mesh, in_specs=placed, out_specs=P(None, "tile", "freq", None), check_vma=False
    )
```

time: 960 us -> 203 us (0.21)
  other arithmetic: 333 us -> 2.78 us
  starting transfers between devices: 262 us -> 0 us
  local copies, waits for them, and re-layouts: 240 us -> 4.97 us
  Pallas kernels: 0 us -> 192 us
  blocking collectives: 47.6 us -> 0 us
  waiting for transfers between devices: 45.3 us -> 0 us
  between operations: 14.4 us -> 0.69 us
  loops' own time: 12.2 us -> 0 us
    ppermute x48 -> x0, starting transfers between devices: 239 us -> none  [from_behind(): return lax.ppermute(array, axis, pairs)]
    pallas_call x0 -> x3, Pallas kernels: none -> 192 us  [the longest x1 114 us: local(): pl.pallas_call(relax_kernel, name='relax_tile', out_shape=jax.ShapeDtypeS...]
    slice x33 -> x0, local copies, waits for them, and re-layouts: 92.4 us -> none  [the longest x24 63.8 us: grow_rims(): lax.slice_in_dim(values, extent - rim_width, extent, axis=direction + 1)]
    scatter-add x3 -> x0, other arithmetic: 76 us -> none  [local(): source = jnp.zeros((3, cell_total), jnp.float32).at[:, got_cells.reshape(...]
    concatenate x16 -> x0, other arithmetic: 72.1 us -> none  [grow_rims(): jnp.concatenate([from_lower, values, from_upper], axis=direction + 1)]
    unnamed x9, local copies, waits for them, and re-layouts: 70.6 us -> 4.97 us
    another operation x12 -> x0, other arithmetic: 56.1 us -> none  [the longest x8 54.5 us: curl_curl(): jnp.stack([backward_step(swirl_z, 1) - backward_step(swirl_y, 2), backwar...]
    add x16 -> x0, other arithmetic: 55.7 us -> none  [the longest x8 36.8 us: relax_sweep(): centre + RELAXATION * (source - curl_curl(padded) - damping * centre) / (...]
  transfers between devices with their start and end apart: 51 -> 0, of which waited for: 27 -> 0; matrix products, arithmetic and copies ran while one was open for 10% -> 0% of each run, Pallas kernels for 0% -> 0%
where the time goes in v1:
time: 203 us; the launch traced here: 201 us
  Pallas kernels  192 us (95%)
  local copies, waits for them, and re-layouts  4.97 us (2%)
  other arithmetic  2.78 us (1%)
    pallas_call x1, Pallas kernels, local(): pl.pallas_call(relax_kernel, name='relax_tile', out_shape=jax.ShapeDtypeS...  114 us
    pallas_call x1, Pallas kernels, local(): pl.pallas_call(spread_kernel, name='spread_rows', out_shape=jax.ShapeDtyp...  42 us
    pallas_call x1, Pallas kernels, local(): pl.pallas_call(gather_kernel, name='gather_lists', out_shape=(jax.ShapeDt...  36.3 us
    unnamed x9, local copies, waits for them, and re-layouts  4.97 us

profile of v1, /device:TPU:1, one launch (start us, length us, event | category | flops | bytes accessed | tf_op | source)
XLA Modules:
  0.0 200.9 jit_solution(1218808555835156787)
XLA Ops:
  0.7 0.7 fusion.8
  1.4 0.7 copy.8.res_ref
  2.1 0.0 copy-start
  2.1 1.2 copy-done
  3.3 0.0 copy-start.3
  3.3 0.7 copy-done.3
  4.0 36.3 %gather_lists.1 = (f32[64,8,128]{2,1,0:T(8,128)S(1)}, f32[112,56,128]{2,1,0:T(8,128)S(1)}) custom-call(f32[1,3,1024]{2,1,0:T(4,128)S(1)} %copy.8.res_ref, s32[1,256]{1,0:T(1,128)S(1)} %copy-done.3, f32[1,256]{1,0:T(1,128)S(1)} %bitcast.10, f32[1]{0:T(128)S(6)} %copy.10.lap_ref, f32[64,32,128]{2,1,0:T(8,128)S(1)} %bitcast.9), custom_call_target="tpu_custom_call" | custom-call | tf_op jit(solution)/shard_map/gather_lists/pallas_call | solution.py:393
  40.3 0.0 copy-start.1
  40.3 1.7 copy-done.1
  41.9 0.0 copy-start.2
  41.9 0.7 copy-done.2
  42.6 114.3 %relax_tile.1.part_ref = f32[64,32,128]{2,1,0:T(8,128)} custom-call(f32[64,8,128]{2,1,0:T(8,128)} %copy-done.2, f32[1]{0:T(128)S(6)} %copy.10.lap_ref, f32[112,56,128]{2,1,0:T(8,128)} %copy-done.1, f32[64,32,128]{2,1,0:T(8,128)} %bitcast.8, bf16[3,64,32,128]{3,2,1,0:T(8,128)(2,1)} %bitcast.11), custom_call_target="tpu_custom_call" | custom-call | tf_op jit(solution)/shard_map/relax_tile/pallas_call | solution.py:414
  156.9 42.0 %spread_rows.1 = f32[128,16,128]{2,1,0:T(8,128)} custom-call(f32[64,32,128]{2,1,0:T(8,128)} %relax_tile.1.part_ref), custom_call_target="tpu_custom_call" | custom-call | tf_op jit(solution)/shard_map/spread_rows/pallas_call | solution.py:434
  198.9 2.1 %add_bitcast_fusion = f32[64,1,16,128]{3,2,1,0:T(8,128)} fusion(f32[128,16,128]{2,1,0:T(8,128)} %spread_rows.1), kind=kLoop, calls=%fused_computation | loop fusion | flops 131072 | bytes 1572864 | tf_op jit(solution)/shard_map/broadcast_in_dim | solution.py:443
Async XLA Ops:
  2.1 1.2 copy-start
  3.3 0.7 copy-start.3
  40.3 1.7 copy-start.1
  41.9 0.7 copy-start.2

commit v2 on v1

--- a/solution.py
+++ b/solution.py
@@ -15,13 +15,14 @@
 TX, TY, TZ = 4, 4, 4
 TILES = 64
 CX, CY, CZ = 64, 32, 128
+NP = 4
 RIM = 7
 
 YR = 56
 B0 = 81
 RUN = 26
 SEG = 42
-PLANES = 112
+PLANES = 116
 OWN = 8
 
 
@@ -60,8 +61,41 @@
     return total
 
 
-def gather_kernel(res_ref, cnt_ref, idx_ref, lap_ref, cond_ref, list_ref, coef_ref,
-                  cext, pack, low, high, sends, recvs, zsend, zrecv, gsend, grecv, lsem):
+def locate(code, tx, ty, tz):
+    x = (code >> 16) - tx * CX + RIM
+    y = ((code >> 9) & 127) - ty * CY + RIM
+    z = (code & 511) - tz * CZ
+    ok = (x >= 0) & (x < CX + 2 * RIM) & (y >= 0) & (y < CY + 2 * RIM) & (z >= -RIM) & (z < CZ + RIM)
+    run = (x >= RUN).astype(I32) + (x >= 2 * RUN).astype(I32)
+    in_a = (z >= 0) & (z < CZ)
+    plane = jnp.where(in_a, x + 1, x - RUN * run + B0)
+    lane = jnp.where(in_a, z, SEG * run + jnp.where(z < 0, z + 7, z - 93))
+    return ok, jnp.where(ok, (plane * YR + y + 1) * 128 + lane, 0).astype(F32)
+
+
+def find_all(list_ref, spots, t):
+    code = jnp.concatenate([list_ref[:, 3, :], list_ref[:, 7, :]], axis=1).astype(I32)
+    ok, spot = locate(code, *place(t))
+    before = (iota((256, 256), 0) < iota((256, 256), 1)).astype(F32).astype(BF16)
+    flag = ok.astype(F32)
+    rank = jnp.dot(flag.astype(BF16), before, preferred_element_type=F32)
+    spots[0] = spot
+    spots[1] = jnp.where(ok, rank, -1.0)
+    return jnp.broadcast_to(jnp.sum(flag, axis=1, keepdims=True), (TILES, 128)).astype(I32)
+
+
+def squeeze(list_ref, spots, b, first):
+    place_k = iota((128, 256), 0).astype(F32)
+    values = jnp.concatenate([list_ref[b, pl.ds(0, 3), :], list_ref[b, pl.ds(4, 3), :]], axis=1)
+    both = jnp.concatenate([values, spots[0, pl.ds(b, 1), :]], axis=0)
+    pick = (place_k == spots[1, pl.ds(b, 1), :] - first).astype(F32).astype(BF16)
+    parts = jnp.concatenate([part.astype(F32) for part in three(both)] + [jnp.zeros((4, 256), F32)], axis=0).astype(BF16)
+    got = lax.dot_general(parts, pick, (((1,), (1,)), ((), ())), preferred_element_type=F32)
+    return (got[0:4] + got[4:8]) + got[8:12]
+
+
+def gather_kernel(res_hbm, cnt_hbm, idx_hbm, lap_ref, cond_ref, list_ref, coef_ref, short_ref, many_ref,
+                  res_ref, cnt_ref, idx_ref, spots, cext, pack, low, high, sends, recvs, zsend, zrecv, gsend, grecv, lsem):
     f, t = lax.axis_index("freq"), lax.axis_index("tile")
     tx, ty, tz = place(t)
     barrier = pltpu.get_barrier_semaphore()
@@ -71,8 +105,14 @@
         return c
 
     lax.fori_loop(1, TILES, greet, 0)
-    own = pltpu.make_async_copy(cond_ref, cext.at[pl.ds(OWN, CX), pl.ds(8, CY)], lsem)
+    own = pltpu.make_async_copy(cond_ref, cext.at[pl.ds(OWN, CX), pl.ds(8, CY)], lsem.at[0])
     own.start()
+    loads = [pltpu.make_async_copy(a, b, lsem.at[n + 1])
+             for n, (a, b) in enumerate(((res_hbm, res_ref), (cnt_hbm, cnt_ref), (idx_hbm, idx_ref)))]
+    for copy in loads:
+        copy.start()
+    for copy in loads:
+        copy.wait()
 
     counts = cnt_ref[...].astype(F32)
     upto = (iota((256, 256), 0) <= iota((256, 256), 1)).astype(F32)
@@ -97,7 +137,7 @@
     lax.fori_loop(1, TILES, share, 0)
 
     spans = {1: (CX - 7, 1, 7), -1: (0, 72, 7), 0: (0, 8, CX)}
-    rows = {1: (CY - 8, 0, 8), -1: (0, 40, 8), 0: (0, 8, CY)}
+    rows = {1: (CY - 7, 1, 7), -1: (0, 40, 7), 0: (0, 8, CY)}
     ways = [(dx, dy) for dx in (-1, 0, 1) for dy in (-1, 0, 1) if (dx, dy) != (0, 0)]
 
     def inside(dx, dy):
@@ -116,6 +156,18 @@
         @pl.when(inside(dx, dy))
         def _(n=n):
             halo(n).start()
+
+    everyone = list_ref.at[pl.ds(0, TILES - 1)]
+    pltpu.make_async_copy(everyone, everyone, grecv).wait()
+    many_ref[...] = find_all(list_ref, spots, t)
+
+    def compact(k, c):
+        for i in range(2):
+            parts = [squeeze(list_ref, spots, 4 * k + 2 * i + j, 0.0) for j in range(2)]
+            short_ref[2 * k + i] = jnp.concatenate(parts, axis=0)
+        return c
+
+    lax.fori_loop(0, TILES // 4, compact, 0)
     own.wait()
     for n, (dx, dy) in enumerate(ways):
         @pl.when(inside(-dx, -dy))
@@ -125,11 +177,19 @@
     def read(i):
         return cext[i]
 
+    lane = iota((48, 128), 1)
+
     def fill(s, c):
-        pack[s] = pack_own(read, s, 48, ((0, 7, -121), (35, 42, 35)))
-        return c
-
-    lax.fori_loop(0, RUN, fill, 0)
+        total = jnp.zeros((48, 128), F32)
+        for h in range(8):
+            plane = cext[jnp.minimum(1 + 10 * h + s, 79)]
+            for begin, shift in ((16 * h, 16 * h - 121), (16 * h + 8, 16 * h + 8)):
+                moved = pltpu.roll(plane, shift % 128, 1)
+                total = jnp.where((lane >= begin) & (lane < begin + 7), moved, total)
+        pack[s] = total
+        return c
+
+    lax.fori_loop(0, 10, fill, 0)
 
     def rim(up):
         return pltpu.make_async_remote_copy(
@@ -164,7 +224,6 @@
     def _():
         rim(0).wait_recv()
 
-    lane = iota((48, 128), 1)
     run = (lane >= SEG).astype(I32) + (lane >= 2 * SEG).astype(I32)
     seg = lane - run * SEG
     z = jnp.where(seg < 21, seg - 7, seg + 93) + tz * CZ
@@ -172,7 +231,14 @@
 
     def fill_b(s, c):
         value = pack_own(read, s, 48, ((7, 21, 7), (21, 35, -93)))
-        value = jnp.where(seg < 7, low[s], jnp.where(seg >= 35, high[s], value))
+        for g in range(3):
+            i = RUN * g + s
+            h = i // 10
+            turn = (SEG * g - 16 * h + 256) % 128
+            from_low = pltpu.roll(low[i - 10 * h], turn, 1)
+            from_high = pltpu.roll(high[i - 10 * h], (turn + 27) % 128, 1)
+            value = jnp.where((lane >= SEG * g) & (lane < SEG * g + 7), from_low, value)
+            value = jnp.where((lane >= SEG * g + 35) & (lane < SEG * g + 42), from_high, value)
         x = RUN * run + s - 7 + tx * CX
         good = yin & zin & (x >= 0) & (x < TX * CX)
         coef_ref[B0 + s, pl.ds(0, 48), :] = jnp.where(good, 1.0 / (4.0 + lap * value), 0.0)
@@ -193,9 +259,7 @@
     def _():
         rim(0).wait_send()
 
-    everyone = list_ref.at[pl.ds(0, TILES - 1)]
     pltpu.make_async_copy(everyone, everyone, gsend).wait()
-    pltpu.make_async_copy(everyone, everyone, grecv).wait()
 
 
 def stencil(src, dst, base, coef, hx_ref, hy_ref, hz_ref, lo, hi, y0, nk, nh, scale):
@@ -214,30 +278,31 @@
         kx = (hz - hz_ref[x, kl, :]) - (hy - pltpu.roll(hy, 1, 1))
         ky = (hx - pltpu.roll(hx, 1, 1)) - (hz - hz_ref[x - 1, kr, :])
         kz = (hy - hy_ref[x - 1, kr, :]) - (hx - hx_ref[x, kl, :])
-        c = coef[x, kr, :]
-        keep = 1.0 + 4.0 * c
+        c = coef[x, kr, :] if scale == 1.0 else scale * coef[x, kr, :]
+        keep = (scale if base is not src else 1.0 + scale) + 4.0 * c
         for i, k in enumerate((kx, ky, kz)):
             new = keep * src[i, x, kr, :] - c * k
-            if base is not None:
-                new = base[i, x, kr, :] + scale * new
+            if base is not None and base is not src:
+                new = base[i, x, kr, :] + new
             dst[i, x, kr, :] = new
 
-    swirl(lo - 1)
-    swirl(lo)
-
-    def body(x, c):
-        relax(x)
-        swirl(x + 1)
-        return c
-
-    lax.fori_loop(lo, hi, body, 0)
-
-
-def relax_kernel(list_ref, lap_ref, coef_hbm, cond_hbm, field_hbm, out_ref,
-                 u, p, q, hx_ref, hy_ref, hz_ref, coef, cond, field, spots, vals, val_s, cnt_s,
-                 sems, cnt_v):
+    for i in range(-1, NP):
+        swirl(lo + i)
+
+    def body(k, c):
+        x = jnp.minimum(lo + NP * k, hi - NP)
+        for i in range(NP):
+            relax(x + i)
+        for i in range(NP):
+            swirl(x + NP + i)
+        return c
+
+    lax.fori_loop(0, (hi - lo + NP - 1) // NP, body, 0)
+
+
+def relax_kernel(list_hbm, lap_ref, short_s, many_s, coef_hbm, cond_hbm, field_hbm, out_ref,
+                 u, p, q, hx_ref, hy_ref, hz_ref, coef, cond, field, list_ref, spots, more, more_s, sems):
     t = lax.axis_index("tile")
-    tx, ty, tz = place(t)
     loads = [pltpu.make_async_copy(a, b, sems.at[n])
              for n, (a, b) in enumerate(((coef_hbm, coef), (cond_hbm, cond), (field_hbm, field)))]
     for copy in loads:
@@ -251,64 +316,67 @@
         return c
 
     lax.fori_loop(0, PLANES, clear, 0)
-
-    before = (iota((128, 128), 0) < iota((128, 128), 1)).astype(F32).astype(BF16)
-    for half in range(2):
-        code = list_ref[:, 4 * half + 3, :].astype(I32)
-        x = (code >> 16) - tx * CX + RIM
-        y = ((code >> 9) & 127) - ty * CY + RIM
-        z = (code & 511) - tz * CZ
-        ok = (x >= 0) & (x < CX + 2 * RIM) & (y >= 0) & (y < CY + 2 * RIM) & (z >= -RIM) & (z < CZ + RIM)
-        run = (x >= RUN).astype(I32) + (x >= 2 * RUN).astype(I32)
-        in_a = (z >= 0) & (z < CZ)
-        plane = jnp.where(in_a, x + 1, x - RUN * run + B0)
-        lane = jnp.where(in_a, z, SEG * run + jnp.where(z < 0, z + 7, z - 93))
-        spot = (plane * YR + y + 1) * 128 + lane
-        flag = ok.astype(F32)
-        rank = jnp.dot(flag.astype(BF16), before, preferred_element_type=F32)
-        spots[half, 0] = jnp.where(ok, spot, 0).astype(F32)
-        spots[half, 1] = jnp.where(ok, rank, -1.0)
-        cnt_v[half] = jnp.broadcast_to(jnp.sum(flag, axis=1, keepdims=True), (TILES, 128)).astype(I32)
-    place_k = iota((128, 128), 0).astype(F32)
-
-    def squeeze(b, c):
-        for half in range(2):
-            values = list_ref[b, pl.ds(4 * half, 3), :]
-            both = jnp.concatenate([values, spots[half, 0, pl.ds(b, 1), :]], axis=0)
-            pick = (place_k == spots[half, 1, pl.ds(b, 1), :]).astype(F32).astype(BF16)
-            got = jnp.zeros((4, 128), F32)
-            for part in three(both):
-                got = got + lax.dot_general(part, pick, (((1,), (1,)), ((), ())), preferred_element_type=F32)
-            vals[2 * b + half] = jnp.concatenate([got, jnp.zeros((4, 128), F32)], axis=0)
-        return c
-
-    lax.fori_loop(0, TILES, squeeze, 0)
-    to_s = [pltpu.make_async_copy(vals, val_s, sems.at[3]), pltpu.make_async_copy(cnt_v, cnt_s, sems.at[4])]
-    for copy in to_s:
+    lane_id = iota((1, 128), 1)
+
+    def add(ref, j, at, count):
+        def four(k, c):
+            rows, gains = [], []
+            for i in range(4):
+                spot = ref[j, at + 3, 4 * k + i].astype(I32)
+                rows.append(spot >> 7)
+                here = lane_id == (spot & 127)
+                gains.append([jnp.where(here, ref[j, at + n, 4 * k + i], 0.0) for n in range(3)])
+            held = [[flat[n, pl.ds(row, 1), :] for n in range(3)] for row in rows]
+            for i in range(4):
+                for n in range(3):
+                    total = held[i][n] + gains[i][n]
+                    for m in range(i):
+                        total = total + jnp.where(rows[m] == rows[i], gains[m][n], 0.0)
+                    held[i][n] = total
+            for i in range(4):
+                for n in range(3):
+                    flat[n, pl.ds(rows[i], 1), :] = held[i][n]
+            return c
+
+        lax.fori_loop(0, (count + 3) // 4, four, 0)
+
+    def drop(k, most):
+        for i in range(2):
+            count = many_s[2 * k + i, 0]
+            add(short_s, k, 4 * i, jnp.minimum(count, 128))
+            most = jnp.maximum(most, count)
+        return most
+
+    most = lax.fori_loop(0, TILES // 2, drop, 0)
+
+    @pl.when(most > 128)
+    def _():
+        copy = pltpu.make_async_copy(list_hbm, list_ref, sems.at[3])
         copy.start()
-    for copy in to_s:
         copy.wait()
-    lane_id = iota((1, 128), 1)
-
-    def drop(b, c):
-        def one(k, c2):
-            spot = val_s[b, 3, k].astype(I32)
-            row, lane = spot >> 7, spot & 127
-            here = lane_id == lane
-            for i in range(3):
-                flat[i, pl.ds(row, 1), :] += jnp.where(here, val_s[b, i, k], 0.0)
-            return c2
-
-        lax.fori_loop(0, cnt_s[b % 2, b // 2, 0], one, 0)
-        return c
-
-    lax.fori_loop(0, 2 * TILES, drop, 0)
+        find_all(list_ref, spots, t)
+
+        def rest(b, c):
+            count = many_s[b, 0] - 128
+
+            @pl.when(count > 0)
+            def _():
+                more[0] = jnp.concatenate([squeeze(list_ref, spots, b, 128.0), jnp.zeros((4, 128), F32)], axis=0)
+                copy = pltpu.make_async_copy(more, more_s, sems.at[3])
+                copy.start()
+                copy.wait()
+                add(more_s, 0, 0, count)
+
+            return c
+
+        lax.fori_loop(0, TILES, rest, 0)
+
     loads[0].wait()
 
     def scale_b(s, c):
         for i in range(3):
-            value = pack_own(lambda k: u[i, k], s, YR, ((7, 21, 7), (21, 35, -93))) + u[i, B0 + s]
-            u[i, B0 + s] = 0.5 * coef[B0 + s] * value
+            value = pack_own(lambda k: u[i, k, pl.ds(0, 48), :], s, 48, ((7, 21, 7), (21, 35, -93))) + u[i, B0 + s, pl.ds(0, 48), :]
+            u[i, B0 + s, pl.ds(0, 48), :] = 0.5 * coef[B0 + s, pl.ds(0, 48), :] * value
         return c
 
     lax.fori_loop(0, RUN, scale_b, 0)
@@ -390,24 +458,29 @@
     codes = ((gx * (TY * CY) + gy) * (TZ * CZ) + gz).astype(F32)[None]
     smem = pl.BlockSpec(memory_space=pltpu.SMEM)
     cond = conductivity[0]
-    lists, coef = pl.pallas_call(
+    lists, coef, short, many = pl.pallas_call(
         gather_kernel,
         name="gather_lists",
-        out_shape=(jax.ShapeDtypeStruct((TILES, 8, 128), F32), jax.ShapeDtypeStruct((PLANES, YR, 128), F32)),
-        in_specs=[vmem(), vmem(), vmem(), smem, hbm()],
-        out_specs=(vmem(), vmem()),
+        out_shape=(jax.ShapeDtypeStruct((TILES, 8, 128), F32), jax.ShapeDtypeStruct((PLANES, YR, 128), F32),
+                   jax.ShapeDtypeStruct((TILES // 2, 8, 128), F32), jax.ShapeDtypeStruct((TILES, 128), I32)),
+        in_specs=[hbm(), hbm(), hbm(), smem, hbm()],
+        out_specs=(vmem(), vmem(), vmem(), vmem()),
         scratch_shapes=[
+            pltpu.VMEM((1, 3, 1024), F32),
+            pltpu.VMEM((1, 256), I32),
+            pltpu.VMEM((1, 256), F32),
+            pltpu.VMEM((2, TILES, 256), F32),
             pltpu.VMEM((80, 48, 128), F32),
-            pltpu.VMEM((RUN, 48, 128), F32),
-            pltpu.VMEM((RUN, 48, 128), F32),
-            pltpu.VMEM((RUN, 48, 128), F32),
+            pltpu.VMEM((10, 48, 128), F32),
+            pltpu.VMEM((10, 48, 128), F32),
+            pltpu.VMEM((10, 48, 128), F32),
             pltpu.SemaphoreType.DMA((8,)),
             pltpu.SemaphoreType.DMA((8,)),
             pltpu.SemaphoreType.DMA((2,)),
             pltpu.SemaphoreType.DMA((2,)),
             pltpu.SemaphoreType.DMA,
             pltpu.SemaphoreType.DMA,
-            pltpu.SemaphoreType.DMA,
+            pltpu.SemaphoreType.DMA((4,)),
         ],
         compiler_params=pltpu.CompilerParams(collective_id=0, has_side_effects=True, vmem_limit_bytes=32 * 2**20),
     )(residual, row_counts, codes, laplace, cond)
@@ -415,22 +488,21 @@
         relax_kernel,
         name="relax_tile",
         out_shape=jax.ShapeDtypeStruct((CX, CY, CZ), F32),
-        in_specs=[vmem(), smem, hbm(), hbm(), hbm()],
+        in_specs=[hbm(), smem, smem, smem, hbm(), hbm(), hbm()],
         out_specs=vmem(),
         scratch_shapes=[pltpu.VMEM((3, PLANES, YR, 128), F32)] * 3
         + [pltpu.VMEM((PLANES, YR, 128), F32)] * 4
         + [
             pltpu.VMEM((CX, CY, CZ), F32),
             pltpu.VMEM((3, CX, CY, CZ), BF16),
-            pltpu.VMEM((2, 2, TILES, 128), F32),
-            pltpu.VMEM((2 * TILES, 8, 128), F32),
-            pltpu.SMEM((2 * TILES, 8, 128), F32),
-            pltpu.SMEM((2, TILES, 128), I32),
-            pltpu.SemaphoreType.DMA((5,)),
-            pltpu.VMEM((2, TILES, 128), I32),
+            pltpu.VMEM((TILES, 8, 128), F32),
+            pltpu.VMEM((2, TILES, 256), F32),
+            pltpu.VMEM((1, 8, 128), F32),
+            pltpu.SMEM((1, 8, 128), F32),
+            pltpu.SemaphoreType.DMA((4,)),
         ],
         compiler_params=pltpu.CompilerParams(vmem_limit_bytes=58 * 2**20),
-    )(lists, laplace, coef, cond, forward_field[0, 0])
+    )(lists, laplace, short, many, coef, cond, forward_field[0, 0])
     both = pl.pallas_call(
         spread_kernel,
         name="spread_rows",

time: 203 us -> 131 us (0.65)
  Pallas kernels: 192 us -> 120 us
    pallas_call x1, Pallas kernels: 114 us -> 52.8 us  [local(): pl.pallas_call(relax_kernel, name='relax_tile', out_shape=jax.ShapeDtypeS...]
    pallas_call x1, Pallas kernels: 42 us -> 31.9 us  [local(): pl.pallas_call(spread_kernel, name='spread_rows', out_shape=jax.ShapeDtyp...]
    unnamed x9 -> x13, local copies, waits for them, and re-layouts: 4.97 us -> 6.26 us
where the time goes in v2:
time: 131 us; the launch traced here: 130 us
  Pallas kernels  120 us (92%)
  local copies, waits for them, and re-layouts  6.26 us (5%)
  other arithmetic  2.78 us (2%)
    pallas_call x1, Pallas kernels, local(): pl.pallas_call(relax_kernel, name='relax_tile', out_shape=jax.ShapeDtypeS...  52.8 us
    pallas_call x1, Pallas kernels, local(): pl.pallas_call(gather_kernel, name='gather_lists', out_shape=(jax.ShapeDt...  35.6 us
    pallas_call x1, Pallas kernels, local(): pl.pallas_call(spread_kernel, name='spread_rows', out_shape=jax.ShapeDtyp...  31.9 us
    unnamed x13, local copies, waits for them, and re-layouts  6.26 us

profile of v2, /device:TPU:1, one launch (start us, length us, event | category | flops | bytes accessed | tf_op | source)
XLA Modules:
  0.0 130.0 jit_solution(13177883906810737521)
XLA Ops:
  0.7 0.7 fusion.8
  1.4 0.7 copy.8.res_hbm
  2.1 0.0 copy-start
  2.1 1.2 copy-done
  3.3 0.0 copy-start.5
  3.3 0.7 copy-done.5
  4.0 35.6 %gather_lists.1 = (f32[64,8,128]{2,1,0:T(8,128)S(1)}, f32[116,56,128]{2,1,0:T(8,128)S(1)}, f32[32,8,128]{2,1,0:T(8,128)S(1)}, s32[64,128]{1,0:T(8,128)S(1)}) custom-call(f32[1,3,1024]{2,1,0:T(4,128)S(1)} %copy.8.res_hbm, s32[1,256]{1,0:T(1,128)S(1)} %copy-done.5, f32[1,256]{1,0:T(1,128)S(1)} %bitcast.10, f32[1]{0:T(128)S(6)} %copy.10.lap_ref, ...), custom_call_target="tpu_custom_call" | custom-call | tf_op jit(solution)/shard_map/gather_lists/pallas_call | solution.py:461
  39.6 0.0 copy-start.1
  39.6 1.7 %copy-done.1 = f32[116,56,128]{2,1,0:T(8,128)} copy-done((f32[116,56,128]{2,1,0:T(8,128)}, f32[116,56,128]{2,1,0:T(8,128)S(1)}, u32[]{:S(2)}) %copy-start.1) | copy-done | bytes 3325976
  41.3 0.0 copy-start.2
  41.3 0.7 copy-done.2
  42.0 0.0 copy-start.3
  42.0 0.6 copy-done.3
  42.6 0.0 copy-start.4
  42.7 0.6 copy-done.4
  43.3 52.8 %relax_tile.1.part_ref = f32[64,32,128]{2,1,0:T(8,128)} custom-call(f32[64,8,128]{2,1,0:T(8,128)} %copy-done.2, f32[1]{0:T(128)S(6)} %copy.10.lap_ref, f32[32,8,128]{2,1,0:T(8,128)} %copy-done.3, s32[64,128]{1,0:T(8,128)} %copy-done.4, f32[116,56,128]{2,1,0:T(8,128)} %copy-done.1, f32[64,32,128]{2,1,0:T(8,128)} %bitcast.8, bf16[3,64,32,128]{3,2,1,0:T(8,128)(2,1)} %bitcast.11), custom_call_target="tpu_custom_call" | custom-call | tf_op jit(solution)/shard_map/relax_tile/pallas_call | solution.py:487
  96.1 31.9 %spread_rows.1 = f32[128,16,128]{2,1,0:T(8,128)} custom-call(f32[64,32,128]{2,1,0:T(8,128)} %relax_tile.1.part_ref), custom_call_target="tpu_custom_call" | custom-call | tf_op jit(solution)/shard_map/spread_rows/pallas_call | solution.py:506
  127.9 2.1 %add_bitcast_fusion = f32[64,1,16,128]{3,2,1,0:T(8,128)} fusion(f32[128,16,128]{2,1,0:T(8,128)} %spread_rows.1), kind=kLoop, calls=%fused_computation | loop fusion | flops 131072 | bytes 1572864 | tf_op jit(solution)/shard_map/broadcast_in_dim | solution.py:515
Async XLA Ops:
  2.1 1.2 copy-start
  3.3 0.7 copy-start.5
  39.6 1.7 %copy-start.1 = (f32[116,56,128]{2,1,0:T(8,128)}, f32[116,56,128]{2,1,0:T(8,128)S(1)}, u32[]{:S(2)}) copy-start(f32[116,56,128]{2,1,0:T(8,128)S(1)} %get-tuple-element.12.coef_hbm) | copy-start | bytes 9977860
  41.3 0.7 copy-start.2
  42.0 0.6 copy-start.3
  42.6 0.6 copy-start.4

commit v3 on v2

--- a/solution.py
+++ b/solution.py
@@ -20,9 +20,12 @@
 
 YR = 56
 B0 = 81
-RUN = 26
-SEG = 42
-PLANES = 116
+RUN = 20
+SEG = 28
+RUNS = 4
+ZB = CZ + RIM - SEG
+PLANES = 108
+KEEP = 64
 OWN = 8
 
 
@@ -50,14 +53,13 @@
     return hi, mid, low
 
 
-def pack_own(read, s, rows, moves):
+def runs_of(read, s, rows, begin, end, shift):
     lane = iota((rows, 128), 1)
     total = jnp.zeros((rows, 128), F32)
-    for g in range(3):
+    for g in range(RUNS):
         plane = read(1 + RUN * g + s)
-        for begin, end, shift in moves:
-            moved = pltpu.roll(plane, (SEG * g + shift) % 128, 1)
-            total = jnp.where((lane >= SEG * g + begin) & (lane < SEG * g + end), moved, total)
+        moved = pltpu.roll(plane, (SEG * g + shift) % 128, 1)
+        total = jnp.where((lane >= SEG * g + begin) & (lane < SEG * g + end), moved, total)
     return total
 
 
@@ -66,10 +68,10 @@
     y = ((code >> 9) & 127) - ty * CY + RIM
     z = (code & 511) - tz * CZ
     ok = (x >= 0) & (x < CX + 2 * RIM) & (y >= 0) & (y < CY + 2 * RIM) & (z >= -RIM) & (z < CZ + RIM)
-    run = (x >= RUN).astype(I32) + (x >= 2 * RUN).astype(I32)
-    in_a = (z >= 0) & (z < CZ)
+    run = sum((x >= RUN * g).astype(I32) for g in range(1, RUNS))
+    in_a = z < 128 - RIM
     plane = jnp.where(in_a, x + 1, x - RUN * run + B0)
-    lane = jnp.where(in_a, z, SEG * run + jnp.where(z < 0, z + 7, z - 93))
+    lane = jnp.where(in_a, z + RIM, SEG * run + z - ZB)
     return ok, jnp.where(ok, (plane * YR + y + 1) * 128 + lane, 0).astype(F32)
 
 
@@ -81,11 +83,12 @@
     rank = jnp.dot(flag.astype(BF16), before, preferred_element_type=F32)
     spots[0] = spot
     spots[1] = jnp.where(ok, rank, -1.0)
-    return jnp.broadcast_to(jnp.sum(flag, axis=1, keepdims=True), (TILES, 128)).astype(I32)
+    ones = jnp.ones((8, 256), BF16)
+    return lax.dot_general(ones, flag.astype(BF16), (((1,), (1,)), ((), ())), preferred_element_type=F32).astype(I32)
 
 
 def squeeze(list_ref, spots, b, first):
-    place_k = iota((128, 256), 0).astype(F32)
+    place_k = iota((KEEP, 256), 0).astype(F32)
     values = jnp.concatenate([list_ref[b, pl.ds(0, 3), :], list_ref[b, pl.ds(4, 3), :]], axis=1)
     both = jnp.concatenate([values, spots[0, pl.ds(b, 1), :]], axis=0)
     pick = (place_k == spots[1, pl.ds(b, 1), :] - first).astype(F32).astype(BF16)
@@ -94,7 +97,7 @@
     return (got[0:4] + got[4:8]) + got[8:12]
 
 
-def gather_kernel(res_hbm, cnt_hbm, idx_hbm, lap_ref, cond_ref, list_ref, coef_ref, short_ref, many_ref,
+def gather_kernel(res_hbm, cnt_hbm, idx_hbm, lap_ref, cond_ref, list_ref, coef_ref, short_ref, spot_ref, many_ref,
                   res_ref, cnt_ref, idx_ref, spots, cext, pack, low, high, sends, recvs, zsend, zrecv, gsend, grecv, lsem):
     f, t = lax.axis_index("freq"), lax.axis_index("tile")
     tx, ty, tz = place(t)
@@ -159,15 +162,25 @@
 
     everyone = list_ref.at[pl.ds(0, TILES - 1)]
     pltpu.make_async_copy(everyone, everyone, grecv).wait()
-    many_ref[...] = find_all(list_ref, spots, t)
+    many_ref[:, pl.ds(0, TILES)] = find_all(list_ref, spots, t)
 
     def compact(k, c):
         for i in range(2):
-            parts = [squeeze(list_ref, spots, 4 * k + 2 * i + j, 0.0) for j in range(2)]
-            short_ref[2 * k + i] = jnp.concatenate(parts, axis=0)
+            pair = jnp.concatenate([squeeze(list_ref, spots, 4 * k + 2 * i + j, 0.0) for j in range(2)], axis=1)
+            short_ref[pl.ds(3 * (2 * k + i), 3), :] = pair[0:3]
+            spot_ref[pl.ds(2 * k + i, 1), :] = pair[3:4].astype(I32)
         return c
 
     lax.fori_loop(0, TILES // 4, compact, 0)
+    spot = spot_ref[...]
+    row, turn = spot >> 7, iota((TILES // 2, 128), 1) & 3
+    clash = jnp.zeros((TILES // 2, 128), I32)
+    for d in (1, 2, 3):
+        same = (pltpu.roll(row, d, 1) == row) & (turn >= d) & (row > 0)
+        clash = clash | same.astype(I32)
+    for d in (126, 127):
+        clash = clash | pltpu.roll(clash, d, 1)
+    spot_ref[...] = jnp.where((turn == 0) & (clash > 0), spot + (1 << 24), spot)
     own.wait()
     for n, (dx, dy) in enumerate(ways):
         @pl.when(inside(-dx, -dy))
@@ -175,7 +188,7 @@
             halo(n).wait_recv()
 
     def read(i):
-        return cext[i]
+        return cext[jnp.minimum(i, 79)]
 
     lane = iota((48, 128), 1)
 
@@ -208,37 +221,35 @@
     yrow = iota((48, 128), 0) - 8
     yin = (yrow + ty * CY >= 0) & (yrow + ty * CY < TY * CY)
 
+    @pl.when(tz > 0)
+    def _():
+        rim(1).wait_recv()
+
     def fill_a(i, c):
+        k = jnp.clip(i - 1, 0, 79)
         x = i - 8 + tx * CX
-        good = yin & (x >= 0) & (x < TX * CX)
-        coef_ref[i, pl.ds(0, 48), :] = jnp.where(good, 1.0 / (4.0 + lap * cext[i]), 0.0)
+        from_low = pltpu.roll(low[k % 10], (128 - 16 * (k // 10)) % 128, 1)
+        value = jnp.where(lane < RIM, from_low, pltpu.roll(cext[i], RIM, 1))
+        good = yin & ((lane >= RIM) | (tz > 0)) & (x >= 0) & (x < TX * CX)
+        coef_ref[i, pl.ds(0, 48), :] = jnp.where(good, 1.0 / (4.0 + lap * value), 0.0)
         return c
 
     lax.fori_loop(0, 80, fill_a, 0)
 
-    @pl.when(tz > 0)
-    def _():
-        rim(1).wait_recv()
-
     @pl.when(tz < TZ - 1)
     def _():
         rim(0).wait_recv()
 
-    run = (lane >= SEG).astype(I32) + (lane >= 2 * SEG).astype(I32)
-    seg = lane - run * SEG
-    z = jnp.where(seg < 21, seg - 7, seg + 93) + tz * CZ
-    zin = (z >= 0) & (z < TZ * CZ) & (lane < 3 * SEG)
+    run = sum((lane >= SEG * g).astype(I32) for g in range(1, RUNS))
+    z = lane - run * SEG + ZB
+    zin = ((z < CZ) | (tz < TZ - 1)) & (lane < RUNS * SEG)
 
     def fill_b(s, c):
-        value = pack_own(read, s, 48, ((7, 21, 7), (21, 35, -93)))
-        for g in range(3):
+        value = runs_of(read, s, 48, 0, SEG - RIM, 128 - ZB)
+        for g in range(RUNS):
             i = RUN * g + s
-            h = i // 10
-            turn = (SEG * g - 16 * h + 256) % 128
-            from_low = pltpu.roll(low[i - 10 * h], turn, 1)
-            from_high = pltpu.roll(high[i - 10 * h], (turn + 27) % 128, 1)
-            value = jnp.where((lane >= SEG * g) & (lane < SEG * g + 7), from_low, value)
-            value = jnp.where((lane >= SEG * g + 35) & (lane < SEG * g + 42), from_high, value)
+            from_high = pltpu.roll(high[i % 10], (SEG * g + SEG - RIM - 8 - 16 * (i // 10) + 256) % 128, 1)
+            value = jnp.where((lane >= SEG * g + SEG - RIM) & (lane < SEG * g + SEG), from_high, value)
         x = RUN * run + s - 7 + tx * CX
         good = yin & zin & (x >= 0) & (x < TX * CX)
         coef_ref[B0 + s, pl.ds(0, 48), :] = jnp.where(good, 1.0 / (4.0 + lap * value), 0.0)
@@ -300,8 +311,8 @@
     lax.fori_loop(0, (hi - lo + NP - 1) // NP, body, 0)
 
 
-def relax_kernel(list_hbm, lap_ref, short_s, many_s, coef_hbm, cond_hbm, field_hbm, out_ref,
-                 u, p, q, hx_ref, hy_ref, hz_ref, coef, cond, field, list_ref, spots, more, more_s, sems):
+def relax_kernel(list_hbm, lap_ref, short_s, spot_s, many_s, coef_hbm, cond_hbm, field_hbm, out_ref,
+                 u, p, q, hx_ref, hy_ref, hz_ref, coef, cond, field, list_ref, spots, more, more_i, more_s, more_is, sems):
     t = lax.axis_index("tile")
     loads = [pltpu.make_async_copy(a, b, sems.at[n])
              for n, (a, b) in enumerate(((coef_hbm, coef), (cond_hbm, cond), (field_hbm, field)))]
@@ -318,38 +329,43 @@
     lax.fori_loop(0, PLANES, clear, 0)
     lane_id = iota((1, 128), 1)
 
-    def add(ref, j, at, count):
+    def add(ref, spot_in, at, at_spot, step, count):
         def four(k, c):
-            rows, gains = [], []
-            for i in range(4):
-                spot = ref[j, at + 3, 4 * k + i].astype(I32)
-                rows.append(spot >> 7)
-                here = lane_id == (spot & 127)
-                gains.append([jnp.where(here, ref[j, at + n, 4 * k + i], 0.0) for n in range(3)])
-            held = [[flat[n, pl.ds(row, 1), :] for n in range(3)] for row in rows]
-            for i in range(4):
-                for n in range(3):
-                    total = held[i][n] + gains[i][n]
-                    for m in range(i):
-                        total = total + jnp.where(rows[m] == rows[i], gains[m][n], 0.0)
-                    held[i][n] = total
-            for i in range(4):
-                for n in range(3):
-                    flat[n, pl.ds(rows[i], 1), :] = held[i][n]
+            first, where = at + 4 * k, at_spot + 4 * k
+            raw = [spot_in[where + i] for i in range(4)]
+            clash = raw[0] >= 1 << 24
+            raw[0] = raw[0] & ((1 << 24) - 1)
+            rows = [value >> 7 for value in raw]
+            here = [lane_id == (value & 127) for value in raw]
+            gains = [[jnp.where(here[i], ref[first + n * step + i], 0.0) for n in range(3)] for i in range(4)]
+
+            @pl.when(clash)
+            def _():
+                for i in range(4):
+                    for n in range(3):
+                        flat[n, pl.ds(rows[i], 1), :] += gains[i][n]
+
+            @pl.when(jnp.logical_not(clash))
+            def _():
+                sums = [[flat[n, pl.ds(rows[i], 1), :] + gains[i][n] for n in range(3)] for i in range(4)]
+                for i in range(4):
+                    for n in range(3):
+                        flat[n, pl.ds(rows[i], 1), :] = sums[i][n]
+
             return c
 
         lax.fori_loop(0, (count + 3) // 4, four, 0)
 
     def drop(k, most):
         for i in range(2):
-            count = many_s[2 * k + i, 0]
-            add(short_s, k, 4 * i, jnp.minimum(count, 128))
+            count = many_s[0, 2 * k + i]
+            add(short_s, spot_s, 384 * k + KEEP * i, 128 * k + KEEP * i, 128, jnp.minimum(count, KEEP))
             most = jnp.maximum(most, count)
         return most
 
     most = lax.fori_loop(0, TILES // 2, drop, 0)
 
-    @pl.when(most > 128)
+    @pl.when(most > KEEP)
     def _():
         copy = pltpu.make_async_copy(list_hbm, list_ref, sems.at[3])
         copy.start()
@@ -357,17 +373,29 @@
         find_all(list_ref, spots, t)
 
         def rest(b, c):
-            count = many_s[b, 0] - 128
-
-            @pl.when(count > 0)
-            def _():
-                more[0] = jnp.concatenate([squeeze(list_ref, spots, b, 128.0), jnp.zeros((4, 128), F32)], axis=0)
-                copy = pltpu.make_async_copy(more, more_s, sems.at[3])
-                copy.start()
-                copy.wait()
-                add(more_s, 0, 0, count)
-
-            return c
+            count = many_s[0, b]
+
+            def chunk(j, c2):
+                got = squeeze(list_ref, spots, b, (KEEP * j).astype(F32))
+                more[pl.ds(0, 3), pl.ds(0, KEEP)] = got[0:3]
+                spot = got[3:4].astype(I32)
+                more_i[pl.ds(0, 1), pl.ds(0, KEEP)] = spot
+                copies = [pltpu.make_async_copy(more, more_s, sems.at[3]), pltpu.make_async_copy(more_i, more_is, sems.at[4])]
+                for copy in copies:
+                    copy.start()
+                for copy in copies:
+                    copy.wait()
+
+                def one(k, c3):
+                    spot = more_is[0, k] & ((1 << 24) - 1)
+                    here = lane_id == (spot & 127)
+                    for n in range(3):
+                        flat[n, pl.ds(spot >> 7, 1), :] += jnp.where(here, more_s[n, k], 0.0)
+                    return c3
+
+                return lax.fori_loop(0, jnp.minimum(count - KEEP * j, KEEP), one, c2)
+
+            return lax.fori_loop(1, (count + KEEP - 1) // KEEP, chunk, c)
 
         lax.fori_loop(0, TILES, rest, 0)
 
@@ -375,7 +403,7 @@
 
     def scale_b(s, c):
         for i in range(3):
-            value = pack_own(lambda k: u[i, k, pl.ds(0, 48), :], s, 48, ((7, 21, 7), (21, 35, -93))) + u[i, B0 + s, pl.ds(0, 48), :]
+            value = runs_of(lambda k: u[i, jnp.minimum(k, 79), pl.ds(0, 48), :], s, 48, 0, 14, 128 - ZB - RIM) + u[i, B0 + s, pl.ds(0, 48), :]
             u[i, B0 + s, pl.ds(0, 48), :] = 0.5 * coef[B0 + s, pl.ds(0, 48), :] * value
         return c
 
@@ -404,19 +432,22 @@
     lane = iota((CY, 128), 1)
     own_y = pl.ds(8, CY)
     lap = lap_ref[0]
-    for g, (begin, end) in enumerate(((0, 19), (19, 45), (45, 64))):
-        def combine(x, c, g=g):
-            total = jnp.zeros((CY, 128), F32)
-            for i in range(3):
-                rims = q[i, B0 + x + RIM - RUN * g, own_y, :]
-                value = jnp.where(lane < RIM, pltpu.roll(rims, (-(SEG * g + 7)) % 128, 1),
-                                  jnp.where(lane >= CZ - RIM, pltpu.roll(rims, (93 - SEG * g) % 128, 1),
-                                            q[i, OWN + x, own_y, :]))
-                total = total + field[i, x].astype(F32) * value
-            out_ref[x] = -lap * cond[x] * total
+    for g in range(RUNS):
+        begin, end = max(0, RUN * g - RIM), min(CX, RUN * (g + 1) - RIM)
+
+        def combine(k, c, g=g, begin=begin, end=end):
+            for j in range(2):
+                x = jnp.minimum(begin + 2 * k + j, end - 1)
+                total = jnp.zeros((CY, 128), F32)
+                for i in range(3):
+                    rims = q[i, B0 + x + RIM - RUN * g, own_y, :]
+                    value = jnp.where(lane >= CZ - 2 * RIM, pltpu.roll(rims, (ZB - SEG * g) % 128, 1),
+                                      pltpu.roll(q[i, OWN + x, own_y, :], 128 - RIM, 1))
+                    total = total + field[i, x].astype(F32) * value
+                out_ref[x] = -lap * cond[x] * total
             return c
 
-        lax.fori_loop(begin, end, combine, 0)
+        lax.fori_loop(0, (end - begin + 1) // 2, combine, 0)
 
 
 def spread_kernel(part_ref, out_ref, send, recv, lsem):
@@ -424,12 +455,8 @@
     me = f * TILES + t
     barrier = pltpu.get_barrier_semaphore()
 
-    def peer(i):
-        d = (me + i) % (2 * TILES)
-        return d // TILES, d % TILES
-
     def greet(i, c):
-        pl.semaphore_signal(barrier, inc=1, device_id=peer(i), device_id_type=MESH)
+        pl.semaphore_signal(barrier, inc=1, device_id=me ^ i, device_id_type=pl.DeviceIdType.LOGICAL)
         return c
 
     lax.fori_loop(1, 2 * TILES, greet, 0)
@@ -438,9 +465,9 @@
     pl.semaphore_wait(barrier, 2 * TILES - 1)
 
     def share(i, c):
-        df, dt = peer(i)
-        pltpu.make_async_remote_copy(part_ref.at[dt, pl.ds(df * 16, 16)], out_ref.at[me], send, recv,
-                                     device_id=(df, dt), device_id_type=MESH).start()
+        d = me ^ i
+        pltpu.make_async_remote_copy(part_ref.at[d & (TILES - 1), pl.ds((d >> 6) * 16, 16)], out_ref.at[me], send, recv,
+                                     device_id=d, device_id_type=pl.DeviceIdType.LOGICAL).start()
         return c
 
     lax.fori_loop(1, 2 * TILES, share, 0)
@@ -458,13 +485,14 @@
     codes = ((gx * (TY * CY) + gy) * (TZ * CZ) + gz).astype(F32)[None]
     smem = pl.BlockSpec(memory_space=pltpu.SMEM)
     cond = conductivity[0]
-    lists, coef, short, many = pl.pallas_call(
+    lists, coef, short, spot, many = pl.pallas_call(
         gather_kernel,
         name="gather_lists",
         out_shape=(jax.ShapeDtypeStruct((TILES, 8, 128), F32), jax.ShapeDtypeStruct((PLANES, YR, 128), F32),
-                   jax.ShapeDtypeStruct((TILES // 2, 8, 128), F32), jax.ShapeDtypeStruct((TILES, 128), I32)),
+                   jax.ShapeDtypeStruct((3 * TILES // 2, 128), F32), jax.ShapeDtypeStruct((TILES // 2, 128), I32),
+                   jax.ShapeDtypeStruct((8, 128), I32)),
         in_specs=[hbm(), hbm(), hbm(), smem, hbm()],
-        out_specs=(vmem(), vmem(), vmem(), vmem()),
+        out_specs=(vmem(), vmem(), vmem(), vmem(), vmem()),
         scratch_shapes=[
             pltpu.VMEM((1, 3, 1024), F32),
             pltpu.VMEM((1, 256), I32),
@@ -482,13 +510,13 @@
             pltpu.SemaphoreType.DMA,
             pltpu.SemaphoreType.DMA((4,)),
         ],
-        compiler_params=pltpu.CompilerParams(collective_id=0, has_side_effects=True, vmem_limit_bytes=32 * 2**20),
+        compiler_params=pltpu.CompilerParams(collective_id=0, has_side_effects=True, vmem_limit_bytes=62 * 2**20),
     )(residual, row_counts, codes, laplace, cond)
     partial = pl.pallas_call(
         relax_kernel,
         name="relax_tile",
         out_shape=jax.ShapeDtypeStruct((CX, CY, CZ), F32),
-        in_specs=[hbm(), smem, smem, smem, hbm(), hbm(), hbm()],
+        in_specs=[hbm(), smem, smem, smem, smem, hbm(), hbm(), hbm()],
         out_specs=vmem(),
         scratch_shapes=[pltpu.VMEM((3, PLANES, YR, 128), F32)] * 3
         + [pltpu.VMEM((PLANES, YR, 128), F32)] * 4
@@ -497,12 +525,14 @@
             pltpu.VMEM((3, CX, CY, CZ), BF16),
             pltpu.VMEM((TILES, 8, 128), F32),
             pltpu.VMEM((2, TILES, 256), F32),
-            pltpu.VMEM((1, 8, 128), F32),
-            pltpu.SMEM((1, 8, 128), F32),
-            pltpu.SemaphoreType.DMA((4,)),
+            pltpu.VMEM((8, 128), F32),
+            pltpu.VMEM((8, 128), I32),
+            pltpu.SMEM((8, 128), F32),
+            pltpu.SMEM((8, 128), I32),
+            pltpu.SemaphoreType.DMA((5,)),
         ],
-        compiler_params=pltpu.CompilerParams(vmem_limit_bytes=58 * 2**20),
-    )(lists, laplace, short, many, coef, cond, forward_field[0, 0])
+        compiler_params=pltpu.CompilerParams(vmem_limit_bytes=62 * 2**20),
+    )(lists, laplace, short.reshape(-1), spot.reshape(-1), many, coef, cond, forward_field[0, 0])
     both = pl.pallas_call(
         spread_kernel,
         name="spread_rows",
@@ -510,7 +540,7 @@
         in_specs=[hbm()],
         out_specs=hbm(),
         scratch_shapes=[pltpu.SemaphoreType.DMA] * 3,
-        compiler_params=pltpu.CompilerParams(collective_id=1, has_side_effects=True),
+        compiler_params=pltpu.CompilerParams(collective_id=1, has_side_effects=True, vmem_limit_bytes=62 * 2**20),
     )(partial)
     return (both[:TILES] + both[TILES:])[:, None]
 

time: 131 us -> 124 us (0.947)
  local copies, waits for them, and re-layouts: 6.26 us -> 1.32 us
    pallas_call x1, Pallas kernels: 35.6 us -> 43.5 us  [local(): pl.pallas_call(gather_kernel, name='gather_lists', out_shape=(jax.ShapeDt...]
    pallas_call x1, Pallas kernels: 52.8 us -> 47.1 us  [local(): pl.pallas_call(relax_kernel, name='relax_tile', out_shape=jax.ShapeDtypeS...]
    unnamed x13 -> x1, local copies, waits for them, and re-layouts: 6.26 us -> 1.32 us
    pallas_call x1, Pallas kernels: 31.9 us -> 28 us  [local(): pl.pallas_call(spread_kernel, name='spread_rows', out_shape=jax.ShapeDtyp...]
where the time goes in v3:
time: 124 us
  Pallas kernels  119 us (96%)
  other arithmetic  3.37 us (3%)
  local copies, waits for them, and re-layouts  1.32 us (1%)
    pallas_call x1, Pallas kernels, local(): pl.pallas_call(relax_kernel, name='relax_tile', out_shape=jax.ShapeDtypeS...  47.1 us
    pallas_call x1, Pallas kernels, local(): pl.pallas_call(gather_kernel, name='gather_lists', out_shape=(jax.ShapeDt...  43.5 us
    pallas_call x1, Pallas kernels, local(): pl.pallas_call(spread_kernel, name='spread_rows', out_shape=jax.ShapeDtyp...  28 us

profile of v3, /device:TPU:1, one launch (start us, length us, event | category | flops | bytes accessed | tf_op | source)
XLA Modules:
  0.0 124.0 jit_solution(11319195190736723422)
XLA Ops:
  0.7 1.3 %fusion.8 = f32[256]{0:T(256)} fusion(s32[256]{0:T(256)} %param.10, s32[256]{0:T(256)} %bitcast.16), kind=kLoop, calls=%fused_computation.31 | loop fusion | flops 23296 | bytes 3072 | tf_op jit(solution)/shard_map/convert_element_type | solution.py:485
  2.0 1.3 %copy.8.res_hbm = f32[1,3,1024]{2,1,0:T(4,128)} copy(f32[1,3,1024]{2,0,1:T(1,128)} %param.7) | data formatting | bytes 24576 | tf_op args[0]
  3.3 43.5 %gather_lists.1 = (f32[64,8,128]{2,1,0:T(8,128)}, f32[108,56,128]{2,1,0:T(8,128)}, f32[96,128]{1,0:T(8,128)}, s32[32,128]{1,0:T(8,128)}, s32[8,128]{1,0:T(8,128)}) custom-call(f32[1,3,1024]{2,1,0:T(4,128)} %copy.8.res_hbm, s32[1,256]{1,0:T(1,128)} %cnt_hbm.1, f32[1,256]{1,0:T(1,128)} %bitcast.15, f32[1]{0:T(128)S(6)} %copy.10.lap_ref, f32[64,32,128]{2,1,0:T(8,128)} %bitcast.10), custom_call_target="tpu_custom_call" | custom-call | tf_op jit(solution)/shard_map/gather_lists/pallas_call | solution.py:488
  46.8 47.1 %relax_tile.1.part_ref = f32[64,32,128]{2,1,0:T(8,128)} custom-call(f32[64,8,128]{2,1,0:T(8,128)} %get-tuple-element.10.list_hbm, f32[1]{0:T(128)S(6)} %copy.10.lap_ref, f32[12288]{0:T(1024)} %bitcast.13, s32[4096]{0:T(1024)} %bitcast.14, s32[8,128]{1,0:T(8,128)} %get-tuple-element.13.many_s, f32[108,56,128]{2,1,0:T(8,128)} %get-tuple-element.14.coef_hbm, ...), custom_call_target="tpu_custom_call" | custom-call | tf_op jit(solution)/shard_map/relax_tile/pallas_call | solution.py:515
  94.0 28.0 %spread_rows.1 = f32[128,16,128]{2,1,0:T(8,128)} custom-call(f32[64,32,128]{2,1,0:T(8,128)} %relax_tile.1.part_ref), custom_call_target="tpu_custom_call" | custom-call | tf_op jit(solution)/shard_map/spread_rows/pallas_call | solution.py:536
  121.9 2.1 %add_bitcast_fusion = f32[64,1,16,128]{3,2,1,0:T(8,128)} fusion(f32[128,16,128]{2,1,0:T(8,128)} %spread_rows.1), kind=kLoop, calls=%fused_computation | loop fusion | flops 131072 | bytes 1572864 | tf_op jit(solution)/shard_map/broadcast_in_dim | solution.py:545

commit v4 on v3

--- a/solution.py
+++ b/solution.py
@@ -97,21 +97,22 @@
     return (got[0:4] + got[4:8]) + got[8:12]
 
 
-def gather_kernel(res_hbm, cnt_hbm, idx_hbm, lap_ref, cond_ref, list_ref, coef_ref, short_ref, spot_ref, many_ref,
-                  res_ref, cnt_ref, idx_ref, spots, cext, pack, low, high, sends, recvs, zsend, zrecv, gsend, grecv, lsem):
+def gather_kernel(res_hbm, cnt_hbm, tile_hbm, cell_hbm, lap_ref, cond_ref, list_ref, coef_ref, short_ref, spot_ref, many_ref,
+                  res_ref, cnt_ref, tile_ref, cell_ref, spots, cext, pack, low, high, sends, recvs, zsend, zrecv, gsend, grecv, lsem):
     f, t = lax.axis_index("freq"), lax.axis_index("tile")
+    me = f * TILES + t
     tx, ty, tz = place(t)
     barrier = pltpu.get_barrier_semaphore()
 
     def greet(i, c):
-        pl.semaphore_signal(barrier, inc=1, device_id=(f, (t + i) % TILES), device_id_type=MESH)
+        pl.semaphore_signal(barrier, inc=1, device_id=me ^ i, device_id_type=pl.DeviceIdType.LOGICAL)
         return c
 
     lax.fori_loop(1, TILES, greet, 0)
     own = pltpu.make_async_copy(cond_ref, cext.at[pl.ds(OWN, CX), pl.ds(8, CY)], lsem.at[0])
     own.start()
     loads = [pltpu.make_async_copy(a, b, lsem.at[n + 1])
-             for n, (a, b) in enumerate(((res_hbm, res_ref), (cnt_hbm, cnt_ref), (idx_hbm, idx_ref)))]
+             for n, (a, b) in enumerate(((res_hbm, res_ref), (cnt_hbm, cnt_ref), (tile_hbm, tile_ref), (cell_hbm, cell_ref)))]
     for copy in loads:
         copy.start()
     for copy in loads:
@@ -124,17 +125,23 @@
     at = iota((1024, 256), 0).astype(F32)
     member = ((at >= starts) & (at < ends)).astype(F32).astype(BF16)
     sums = jnp.zeros((3, 256), F32)
-    for part in three(res_ref[0]):
+    for part in three(res_ref[:, 0, :]):
         sums = sums + jnp.dot(part, member, preferred_element_type=F32)
     means = sums / counts
-    both = jnp.concatenate([means, idx_ref[...]], axis=0)
+    owner, cell = tile_ref[...], cell_ref[...]
+    gx = (owner >> 4) * CX + (cell >> 12)
+    gy = ((owner >> 2) & 3) * CY + ((cell >> 7) & 31)
+    gz = (owner & 3) * CZ + (cell & 127)
+    code = ((gx * (TY * CY) + gy) * (TZ * CZ) + gz).astype(F32)
+    both = jnp.concatenate([means, code], axis=0)
     list_ref[t] = jnp.concatenate([both[:, :128], both[:, 128:]], axis=0)
 
+    own.wait()
     pl.semaphore_wait(barrier, TILES - 1)
 
     def share(i, c):
         pltpu.make_async_remote_copy(list_ref.at[t], list_ref.at[t], gsend, grecv,
-                                     device_id=(f, (t + i) % TILES), device_id_type=MESH).start()
+                                     device_id=me ^ i, device_id_type=pl.DeviceIdType.LOGICAL).start()
         return c
 
     lax.fori_loop(1, TILES, share, 0)
@@ -152,7 +159,7 @@
         xs, xd, xn = spans[dx]
         ys, yd, yn = rows[dy]
         return pltpu.make_async_remote_copy(
-            cond_ref.at[pl.ds(xs, xn), pl.ds(ys, yn)], cext.at[pl.ds(xd, xn), pl.ds(yd, yn)],
+            cext.at[pl.ds(OWN + xs, xn), pl.ds(8 + ys, yn)], cext.at[pl.ds(xd, xn), pl.ds(yd, yn)],
             sends.at[n], recvs.at[n], device_id=(f, t + dx * TY * TZ + dy * TZ), device_id_type=MESH)
 
     for n, (dx, dy) in enumerate(ways):
@@ -172,16 +179,6 @@
         return c
 
     lax.fori_loop(0, TILES // 4, compact, 0)
-    spot = spot_ref[...]
-    row, turn = spot >> 7, iota((TILES // 2, 128), 1) & 3
-    clash = jnp.zeros((TILES // 2, 128), I32)
-    for d in (1, 2, 3):
-        same = (pltpu.roll(row, d, 1) == row) & (turn >= d) & (row > 0)
-        clash = clash | same.astype(I32)
-    for d in (126, 127):
-        clash = clash | pltpu.roll(clash, d, 1)
-    spot_ref[...] = jnp.where((turn == 0) & (clash > 0), spot + (1 << 24), spot)
-    own.wait()
     for n, (dx, dy) in enumerate(ways):
         @pl.when(inside(-dx, -dy))
         def _(n=n):
@@ -329,37 +326,25 @@
     lax.fori_loop(0, PLANES, clear, 0)
     lane_id = iota((1, 128), 1)
 
-    def add(ref, spot_in, at, at_spot, step, count):
-        def four(k, c):
-            first, where = at + 4 * k, at_spot + 4 * k
-            raw = [spot_in[where + i] for i in range(4)]
-            clash = raw[0] >= 1 << 24
-            raw[0] = raw[0] & ((1 << 24) - 1)
-            rows = [value >> 7 for value in raw]
-            here = [lane_id == (value & 127) for value in raw]
-            gains = [[jnp.where(here[i], ref[first + n * step + i], 0.0) for n in range(3)] for i in range(4)]
-
-            @pl.when(clash)
-            def _():
-                for i in range(4):
-                    for n in range(3):
-                        flat[n, pl.ds(rows[i], 1), :] += gains[i][n]
-
-            @pl.when(jnp.logical_not(clash))
-            def _():
-                sums = [[flat[n, pl.ds(rows[i], 1), :] + gains[i][n] for n in range(3)] for i in range(4)]
-                for i in range(4):
-                    for n in range(3):
-                        flat[n, pl.ds(rows[i], 1), :] = sums[i][n]
-
-            return c
-
-        lax.fori_loop(0, (count + 3) // 4, four, 0)
-
     def drop(k, most):
         for i in range(2):
             count = many_s[0, 2 * k + i]
-            add(short_s, spot_s, 384 * k + KEEP * i, 128 * k + KEEP * i, 128, jnp.minimum(count, KEEP))
+
+            def read(j, i=i):
+                at, where = 384 * k + KEEP * i + 4 * j, 128 * k + KEEP * i + 4 * j
+                return (tuple(spot_s[where + m] for m in range(4)),
+                        tuple(short_s[at + 128 * n + m] for m in range(4) for n in range(3)))
+
+            def four(j, held):
+                coming = read(j + 1)
+                for m in range(4):
+                    here = lane_id == (held[0][m] & 127)
+                    row = pl.ds(held[0][m] >> 7, 1)
+                    for n in range(3):
+                        flat[n, row, :] += jnp.where(here, held[1][3 * m + n], 0.0)
+                return coming
+
+            lax.fori_loop(0, (jnp.minimum(count, KEEP) + 3) // 4, four, read(0))
             most = jnp.maximum(most, count)
         return most
 
@@ -387,7 +372,7 @@
                     copy.wait()
 
                 def one(k, c3):
-                    spot = more_is[0, k] & ((1 << 24) - 1)
+                    spot = more_is[0, k]
                     here = lane_id == (spot & 127)
                     for n in range(3):
                         flat[n, pl.ds(spot >> 7, 1), :] += jnp.where(here, more_s[n, k], 0.0)
@@ -401,13 +386,18 @@
 
     loads[0].wait()
 
-    def scale_b(s, c):
-        for i in range(3):
-            value = runs_of(lambda k: u[i, jnp.minimum(k, 79), pl.ds(0, 48), :], s, 48, 0, 14, 128 - ZB - RIM) + u[i, B0 + s, pl.ds(0, 48), :]
-            u[i, B0 + s, pl.ds(0, 48), :] = 0.5 * coef[B0 + s, pl.ds(0, 48), :] * value
-        return c
-
-    lax.fori_loop(0, RUN, scale_b, 0)
+    def scale_b(k, c):
+        done = []
+        for j in range(2):
+            s = 2 * k + j
+            for i in range(3):
+                value = runs_of(lambda k: u[i, jnp.minimum(k, 79), pl.ds(0, 48), :], s, 48, 0, 14, 128 - ZB - RIM)
+                done.append((i, B0 + s, 0.5 * coef[B0 + s, pl.ds(0, 48), :] * (value + u[i, B0 + s, pl.ds(0, 48), :])))
+        for i, s, value in done:
+            u[i, s, pl.ds(0, 48), :] = value
+        return c
+
+    lax.fori_loop(0, RUN // 2, scale_b, 0)
 
     def scale_a(k, c):
         for i in range(3):
@@ -436,8 +426,8 @@
         begin, end = max(0, RUN * g - RIM), min(CX, RUN * (g + 1) - RIM)
 
         def combine(k, c, g=g, begin=begin, end=end):
-            for j in range(2):
-                x = jnp.minimum(begin + 2 * k + j, end - 1)
+            for j in range(4):
+                x = jnp.minimum(begin + 4 * k + j, end - 1)
                 total = jnp.zeros((CY, 128), F32)
                 for i in range(3):
                     rims = q[i, B0 + x + RIM - RUN * g, own_y, :]
@@ -447,7 +437,7 @@
                 out_ref[x] = -lap * cond[x] * total
             return c
 
-        lax.fori_loop(0, (end - begin + 1) // 2, combine, 0)
+        lax.fori_loop(0, (end - begin + 3) // 4, combine, 0)
 
 
 def spread_kernel(part_ref, out_ref, send, recv, lsem):
@@ -478,25 +468,21 @@
 
 
 def local(residual, row_counts, recv_owner, recv_cell, conductivity, laplace, forward_field):
-    owner = recv_owner[:, 0]
-    gx = (owner // (TY * TZ)) * CX + recv_cell // (CY * CZ)
-    gy = (owner // TZ % TY) * CY + recv_cell // CZ % CY
-    gz = (owner % TZ) * CZ + recv_cell % CZ
-    codes = ((gx * (TY * CY) + gy) * (TZ * CZ) + gz).astype(F32)[None]
     smem = pl.BlockSpec(memory_space=pltpu.SMEM)
     cond = conductivity[0]
     lists, coef, short, spot, many = pl.pallas_call(
         gather_kernel,
         name="gather_lists",
         out_shape=(jax.ShapeDtypeStruct((TILES, 8, 128), F32), jax.ShapeDtypeStruct((PLANES, YR, 128), F32),
-                   jax.ShapeDtypeStruct((3 * TILES // 2, 128), F32), jax.ShapeDtypeStruct((TILES // 2, 128), I32),
+                   jax.ShapeDtypeStruct((104, 128), F32), jax.ShapeDtypeStruct((40, 128), I32),
                    jax.ShapeDtypeStruct((8, 128), I32)),
-        in_specs=[hbm(), hbm(), hbm(), smem, hbm()],
+        in_specs=[hbm(), hbm(), hbm(), hbm(), smem, hbm()],
         out_specs=(vmem(), vmem(), vmem(), vmem(), vmem()),
         scratch_shapes=[
-            pltpu.VMEM((1, 3, 1024), F32),
+            pltpu.VMEM((3, 1, 1024), F32),
             pltpu.VMEM((1, 256), I32),
-            pltpu.VMEM((1, 256), F32),
+            pltpu.VMEM((1, 256), I32),
+            pltpu.VMEM((1, 256), I32),
             pltpu.VMEM((2, TILES, 256), F32),
             pltpu.VMEM((80, 48, 128), F32),
             pltpu.VMEM((10, 48, 128), F32),
@@ -508,10 +494,10 @@
             pltpu.SemaphoreType.DMA((2,)),
             pltpu.SemaphoreType.DMA,
             pltpu.SemaphoreType.DMA,
-            pltpu.SemaphoreType.DMA((4,)),
+            pltpu.SemaphoreType.DMA((5,)),
         ],
         compiler_params=pltpu.CompilerParams(collective_id=0, has_side_effects=True, vmem_limit_bytes=62 * 2**20),
-    )(residual, row_counts, codes, laplace, cond)
+    )(residual.transpose(1, 0, 2), row_counts, recv_owner.reshape(1, -1), recv_cell.reshape(1, -1), laplace, cond)
     partial = pl.pallas_call(
         relax_kernel,
         name="relax_tile",

time: 124 us -> 117 us (0.944)
  Pallas kernels: 119 us -> 115 us
  local copies, waits for them, and re-layouts: 1.32 us -> 0 us
  other arithmetic: 3.37 us -> 2.06 us
    pallas_call x1, Pallas kernels: 43.5 us -> 36.8 us  [local(): pl.pallas_call(gather_kernel, name='gather_lists', out_shape=(jax.ShapeDt...]
    pallas_call x1, Pallas kernels: 28 us -> 30.2 us  [local(): pl.pallas_call(spread_kernel, name='spread_rows', out_shape=jax.ShapeDtyp...]
    unnamed x1 -> x0, local copies, waits for them, and re-layouts: 1.32 us -> none
    convert_element_type x1 -> x0, other arithmetic: 1.31 us -> none  [local(): codes = ((gx * (TY * CY) + gy) * (TZ * CZ) + gz).astype(F32)[None]]
where the time goes in v4:
time: 117 us
  Pallas kernels  115 us (98%)
  other arithmetic  2.06 us (2%)
    pallas_call x1, Pallas kernels, local(): pl.pallas_call(relax_kernel, name='relax_tile', out_shape=jax.ShapeDtypeS...  47.6 us
    pallas_call x1, Pallas kernels, local(): pl.pallas_call(gather_kernel, name='gather_lists', out_shape=(jax.ShapeDt...  36.8 us
    pallas_call x1, Pallas kernels, local(): pl.pallas_call(spread_kernel, name='spread_rows', out_shape=jax.ShapeDtyp...  30.2 us

profile of v4, /device:TPU:1, one launch (start us, length us, event | category | flops | bytes accessed | tf_op | source)
XLA Modules:
  0.0 117.3 jit_solution(906741906977157815)
XLA Ops:
  0.7 36.8 %gather_lists.1 = (f32[64,8,128]{2,1,0:T(8,128)}, f32[108,56,128]{2,1,0:T(8,128)}, f32[104,128]{1,0:T(8,128)}, s32[40,128]{1,0:T(8,128)}, s32[8,128]{1,0:T(8,128)}) custom-call(f32[3,1,1024]{2,1,0:T(1,128)} %bitcast.16, s32[1,256]{1,0:T(1,128)} %cnt_hbm.1, s32[1,256]{1,0:T(1,128)} %bitcast.17, s32[1,256]{1,0:T(1,128)} %bitcast.18, f32[1]{0:T(128)S(6)} %copy.9.lap_ref, ...), custom_call_target="tpu_custom_call" | custom-call | tf_op jit(solution)/shard_map/gather_lists/pallas_call | solution.py:473
  37.5 47.6 %relax_tile.1.part_ref = f32[64,32,128]{2,1,0:T(8,128)} custom-call(f32[64,8,128]{2,1,0:T(8,128)} %get-tuple-element.10.list_hbm, f32[1]{0:T(128)S(6)} %copy.9.lap_ref, f32[13312]{0:T(1024)} %bitcast.14, s32[5120]{0:T(1024)} %bitcast.15, s32[8,128]{1,0:T(8,128)} %get-tuple-element.13.many_s, f32[108,56,128]{2,1,0:T(8,128)} %get-tuple-element.14.coef_hbm, ...), custom_call_target="tpu_custom_call" | custom-call | tf_op jit(solution)/shard_map/relax_tile/pallas_call | solution.py:501
  85.1 30.2 %spread_rows.1 = f32[128,16,128]{2,1,0:T(8,128)} custom-call(f32[64,32,128]{2,1,0:T(8,128)} %relax_tile.1.part_ref), custom_call_target="tpu_custom_call" | custom-call | tf_op jit(solution)/shard_map/spread_rows/pallas_call | solution.py:522
  115.3 2.1 %add_bitcast_fusion = f32[64,1,16,128]{3,2,1,0:T(8,128)} fusion(f32[128,16,128]{2,1,0:T(8,128)} %spread_rows.1), kind=kLoop, calls=%fused_computation | loop fusion | flops 131072 | bytes 1572864 | tf_op jit(solution)/shard_map/broadcast_in_dim | solution.py:531

commit v5 on v4

--- a/solution.py
+++ b/solution.py
@@ -98,7 +98,7 @@
 
 
 def gather_kernel(res_hbm, cnt_hbm, tile_hbm, cell_hbm, lap_ref, cond_ref, list_ref, coef_ref, short_ref, spot_ref, many_ref,
-                  res_ref, cnt_ref, tile_ref, cell_ref, spots, cext, pack, low, high, sends, recvs, zsend, zrecv, gsend, grecv, lsem):
+                  res_ref, cnt_ref, tile_ref, cell_ref, spots, raw, cext, pack, low, high, sends, recvs, zsend, zrecv, gsend, grecv, lsem):
     f, t = lax.axis_index("freq"), lax.axis_index("tile")
     me = f * TILES + t
     tx, ty, tz = place(t)
@@ -109,7 +109,7 @@
         return c
 
     lax.fori_loop(1, TILES, greet, 0)
-    own = pltpu.make_async_copy(cond_ref, cext.at[pl.ds(OWN, CX), pl.ds(8, CY)], lsem.at[0])
+    own = pltpu.make_async_copy(cond_ref, raw, lsem.at[0])
     own.start()
     loads = [pltpu.make_async_copy(a, b, lsem.at[n + 1])
              for n, (a, b) in enumerate(((res_hbm, res_ref), (cnt_hbm, cnt_ref), (tile_hbm, tile_ref), (cell_hbm, cell_ref)))]
@@ -136,16 +136,6 @@
     both = jnp.concatenate([means, code], axis=0)
     list_ref[t] = jnp.concatenate([both[:, :128], both[:, 128:]], axis=0)
 
-    own.wait()
-    pl.semaphore_wait(barrier, TILES - 1)
-
-    def share(i, c):
-        pltpu.make_async_remote_copy(list_ref.at[t], list_ref.at[t], gsend, grecv,
-                                     device_id=me ^ i, device_id_type=pl.DeviceIdType.LOGICAL).start()
-        return c
-
-    lax.fori_loop(1, TILES, share, 0)
-
     spans = {1: (CX - 7, 1, 7), -1: (0, 72, 7), 0: (0, 8, CX)}
     rows = {1: (CY - 7, 1, 7), -1: (0, 40, 7), 0: (0, 8, CY)}
     ways = [(dx, dy) for dx in (-1, 0, 1) for dy in (-1, 0, 1) if (dx, dy) != (0, 0)]
@@ -162,11 +152,50 @@
             cext.at[pl.ds(OWN + xs, xn), pl.ds(8 + ys, yn)], cext.at[pl.ds(xd, xn), pl.ds(yd, yn)],
             sends.at[n], recvs.at[n], device_id=(f, t + dx * TY * TZ + dy * TZ), device_id_type=MESH)
 
+    for dx, dy in ways:
+        @pl.when(jnp.logical_not(inside(-dx, -dy)))
+        def _(dx=dx, dy=dy):
+            def wipe(i, c):
+                cext[spans[dx][1] + i, pl.ds(rows[dy][1], rows[dy][2]), :] = jnp.zeros((rows[dy][2], 128), F32)
+                return c
+
+            lax.fori_loop(0, spans[dx][2], wipe, 0)
+    lap = lap_ref[0]
+    lane = iota((48, 128), 1)
+    own.wait()
+
+    def invert(k, c):
+        done = [1.0 / (4.0 + lap * raw[4 * k + j]) for j in range(4)]
+        for j in range(4):
+            cext[OWN + 4 * k + j, pl.ds(8, CY), :] = done[j]
+        return c
+
+    lax.fori_loop(0, CX // 4, invert, 0)
+    pl.semaphore_wait(barrier, TILES - 1)
+
+    def share(i, c):
+        pltpu.make_async_remote_copy(list_ref.at[t], list_ref.at[t], gsend, grecv,
+                                     device_id=me ^ i, device_id_type=pl.DeviceIdType.LOGICAL).start()
+        return c
+
+    lax.fori_loop(1, TILES, share, 0)
+
     for n, (dx, dy) in enumerate(ways):
         @pl.when(inside(dx, dy))
         def _(n=n):
             halo(n).start()
 
+    def lay(planes, begin, count):
+        part = pl.ds(begin, count)
+        done = [jnp.where(lane[:count] < RIM, 0.0, pltpu.roll(cext[i, part, :], RIM, 1)) for i in planes]
+        for i, value in zip(planes, done):
+            coef_ref[i, part, :] = value
+
+    def lay_own(k, c):
+        lay([OWN + 4 * k + j for j in range(4)], 8, CY)
+        return c
+
+    lax.fori_loop(0, CX // 4, lay_own, 0)
     everyone = list_ref.at[pl.ds(0, TILES - 1)]
     pltpu.make_async_copy(everyone, everyone, grecv).wait()
     many_ref[:, pl.ds(0, TILES)] = find_all(list_ref, spots, t)
@@ -187,19 +216,21 @@
     def read(i):
         return cext[jnp.minimum(i, 79)]
 
-    lane = iota((48, 128), 1)
-
-    def fill(s, c):
-        total = jnp.zeros((48, 128), F32)
-        for h in range(8):
-            plane = cext[jnp.minimum(1 + 10 * h + s, 79)]
-            for begin, shift in ((16 * h, 16 * h - 121), (16 * h + 8, 16 * h + 8)):
-                moved = pltpu.roll(plane, shift % 128, 1)
-                total = jnp.where((lane >= begin) & (lane < begin + 7), moved, total)
-        pack[s] = total
-        return c
-
-    lax.fori_loop(0, 10, fill, 0)
+    def fill(k, c):
+        done = []
+        for j in range(2):
+            total = jnp.zeros((48, 128), F32)
+            for h in range(8):
+                plane = read(1 + 10 * h + 2 * k + j)
+                for begin, shift in ((16 * h, 16 * h - 121), (16 * h + 8, 16 * h + 8)):
+                    moved = pltpu.roll(plane, shift % 128, 1)
+                    total = jnp.where((lane >= begin) & (lane < begin + 7), moved, total)
+            done.append(total)
+        for j in range(2):
+            pack[2 * k + j] = done[j]
+        return c
+
+    lax.fori_loop(0, 5, fill, 0)
 
     def rim(up):
         return pltpu.make_async_remote_copy(
@@ -214,45 +245,63 @@
     def _():
         rim(0).start()
 
-    lap = lap_ref[0]
-    yrow = iota((48, 128), 0) - 8
-    yin = (yrow + ty * CY >= 0) & (yrow + ty * CY < TY * CY)
+    def lay_rows(k, c):
+        planes = [OWN + 4 * k + j for j in range(4)]
+        lay(planes, 0, 8)
+        lay(planes, 40, 8)
+        return c
+
+    lax.fori_loop(0, CX // 4, lay_rows, 0)
+
+    def lay_planes(k, c):
+        lay([1 + k, 72 + k], 0, 48)
+        return c
+
+    lax.fori_loop(0, RIM, lay_planes, 0)
+
+    def fill_b(k, c):
+        done = [runs_of(read, 2 * k + j, 48, 0, SEG - RIM, 128 - ZB) for j in range(2)]
+        for j in range(2):
+            coef_ref[B0 + 2 * k + j, pl.ds(0, 48), :] = done[j]
+        return c
+
+    lax.fori_loop(0, RUN // 2, fill_b, 0)
 
     @pl.when(tz > 0)
     def _():
         rim(1).wait_recv()
 
-    def fill_a(i, c):
-        k = jnp.clip(i - 1, 0, 79)
-        x = i - 8 + tx * CX
-        from_low = pltpu.roll(low[k % 10], (128 - 16 * (k // 10)) % 128, 1)
-        value = jnp.where(lane < RIM, from_low, pltpu.roll(cext[i], RIM, 1))
-        good = yin & ((lane >= RIM) | (tz > 0)) & (x >= 0) & (x < TX * CX)
-        coef_ref[i, pl.ds(0, 48), :] = jnp.where(good, 1.0 / (4.0 + lap * value), 0.0)
-        return c
-
-    lax.fori_loop(0, 80, fill_a, 0)
+        def patch(k, c):
+            done = []
+            for h in range(8):
+                old = coef_ref[1 + 10 * h + k, pl.ds(0, 48), :]
+                done.append(jnp.where(lane < RIM, pltpu.roll(low[k], (128 - 16 * h) % 128, 1), old))
+            for h in range(8):
+                coef_ref[1 + 10 * h + k, pl.ds(0, 48), :] = done[h]
+            return c
+
+        lax.fori_loop(0, 10, patch, 0)
 
     @pl.when(tz < TZ - 1)
     def _():
         rim(0).wait_recv()
 
-    run = sum((lane >= SEG * g).astype(I32) for g in range(1, RUNS))
-    z = lane - run * SEG + ZB
-    zin = ((z < CZ) | (tz < TZ - 1)) & (lane < RUNS * SEG)
-
-    def fill_b(s, c):
-        value = runs_of(read, s, 48, 0, SEG - RIM, 128 - ZB)
-        for g in range(RUNS):
-            i = RUN * g + s
-            from_high = pltpu.roll(high[i % 10], (SEG * g + SEG - RIM - 8 - 16 * (i // 10) + 256) % 128, 1)
-            value = jnp.where((lane >= SEG * g + SEG - RIM) & (lane < SEG * g + SEG), from_high, value)
-        x = RUN * run + s - 7 + tx * CX
-        good = yin & zin & (x >= 0) & (x < TX * CX)
-        coef_ref[B0 + s, pl.ds(0, 48), :] = jnp.where(good, 1.0 / (4.0 + lap * value), 0.0)
-        return c
-
-    lax.fori_loop(0, RUN, fill_b, 0)
+        def patch(k, c):
+            done = []
+            for j in range(2):
+                s = 2 * k + j
+                value = coef_ref[B0 + s, pl.ds(0, 48), :]
+                for g in range(RUNS):
+                    i = RUN * g + s
+                    turn = (SEG * g + SEG - RIM - 8 - 16 * (i // 10) + 256) % 128
+                    inner = (lane >= SEG * g + SEG - RIM) & (lane < SEG * g + SEG)
+                    value = jnp.where(inner, pltpu.roll(high[i % 10], turn, 1), value)
+                done.append(value)
+            for j in range(2):
+                coef_ref[B0 + 2 * k + j, pl.ds(0, 48), :] = done[j]
+            return c
+
+        lax.fori_loop(0, RUN // 2, patch, 0)
 
     for n, (dx, dy) in enumerate(ways):
         @pl.when(inside(dx, dy))
@@ -484,7 +533,8 @@
             pltpu.VMEM((1, 256), I32),
             pltpu.VMEM((1, 256), I32),
             pltpu.VMEM((2, TILES, 256), F32),
-            pltpu.VMEM((80, 48, 128), F32),
+            pltpu.VMEM((CX, CY, CZ), F32),
+            pltpu.VMEM((82, 48, 128), F32),
             pltpu.VMEM((10, 48, 128), F32),
             pltpu.VMEM((10, 48, 128), F32),
             pltpu.VMEM((10, 48, 128), F32),

time: 117 us -> 111 us (0.949); the launches traced: 117 us -> 113 us
  Pallas kernels: 115 us -> 110 us
    pallas_call x1, Pallas kernels: 30.2 us -> 37.7 us  [local(): pl.pallas_call(spread_kernel, name='spread_rows', out_shape=jax.ShapeDtyp...]
    pallas_call x1, Pallas kernels: 47.6 us -> 41.4 us  [local(): pl.pallas_call(relax_kernel, name='relax_tile', out_shape=jax.ShapeDtypeS...]
    pallas_call x1, Pallas kernels: 36.8 us -> 30.8 us  [local(): pl.pallas_call(gather_kernel, name='gather_lists', out_shape=(jax.ShapeDt...]
where the time goes in v5:
time: 111 us; the launch traced here: 113 us
  Pallas kernels  110 us (99%)
  other arithmetic  2.06 us (2%)
    pallas_call x1, Pallas kernels, local(): pl.pallas_call(relax_kernel, name='relax_tile', out_shape=jax.ShapeDtypeS...  41.4 us
    pallas_call x1, Pallas kernels, local(): pl.pallas_call(spread_kernel, name='spread_rows', out_shape=jax.ShapeDtyp...  37.7 us
    pallas_call x1, Pallas kernels, local(): pl.pallas_call(gather_kernel, name='gather_lists', out_shape=(jax.ShapeDt...  30.8 us

profile of v5, /device:TPU:1, one launch (start us, length us, event | category | flops | bytes accessed | tf_op | source)
XLA Modules:
  0.0 112.7 jit_solution(7245488271941475461)
XLA Ops:
  0.7 30.8 %gather_lists.1 = (f32[64,8,128]{2,1,0:T(8,128)}, f32[108,56,128]{2,1,0:T(8,128)}, f32[104,128]{1,0:T(8,128)}, s32[40,128]{1,0:T(8,128)}, s32[8,128]{1,0:T(8,128)}) custom-call(f32[3,1,1024]{2,1,0:T(1,128)} %bitcast.16, s32[1,256]{1,0:T(1,128)} %cnt_hbm.1, s32[1,256]{1,0:T(1,128)} %bitcast.17, s32[1,256]{1,0:T(1,128)} %bitcast.18, f32[1]{0:T(128)S(6)} %copy.9.lap_ref, ...), custom_call_target="tpu_custom_call" | custom-call | tf_op jit(solution)/shard_map/gather_lists/pallas_call | solution.py:522
  31.5 41.4 %relax_tile.1.part_ref = f32[64,32,128]{2,1,0:T(8,128)} custom-call(f32[64,8,128]{2,1,0:T(8,128)} %get-tuple-element.10.list_hbm, f32[1]{0:T(128)S(6)} %copy.9.lap_ref, f32[13312]{0:T(1024)} %bitcast.14, s32[5120]{0:T(1024)} %bitcast.15, s32[8,128]{1,0:T(8,128)} %get-tuple-element.13.many_s, f32[108,56,128]{2,1,0:T(8,128)} %get-tuple-element.14.coef_hbm, ...), custom_call_target="tpu_custom_call" | custom-call | tf_op jit(solution)/shard_map/relax_tile/pallas_call | solution.py:551
  72.9 37.7 %spread_rows.1 = f32[128,16,128]{2,1,0:T(8,128)} custom-call(f32[64,32,128]{2,1,0:T(8,128)} %relax_tile.1.part_ref), custom_call_target="tpu_custom_call" | custom-call | tf_op jit(solution)/shard_map/spread_rows/pallas_call | solution.py:572
  110.6 2.1 %add_bitcast_fusion = f32[64,1,16,128]{3,2,1,0:T(8,128)} fusion(f32[128,16,128]{2,1,0:T(8,128)} %spread_rows.1), kind=kLoop, calls=%fused_computation | loop fusion | flops 131072 | bytes 1572864 | tf_op jit(solution)/shard_map/broadcast_in_dim | solution.py:581

commit v6 on v5

--- a/solution.py
+++ b/solution.py
@@ -15,7 +15,7 @@
 TX, TY, TZ = 4, 4, 4
 TILES = 64
 CX, CY, CZ = 64, 32, 128
-NP = 4
+NP_A, NP_B = 8, 10
 RIM = 7
 
 YR = 56
@@ -24,7 +24,7 @@
 SEG = 28
 RUNS = 4
 ZB = CZ + RIM - SEG
-PLANES = 108
+PLANES = 112
 KEEP = 64
 OWN = 8
 
@@ -319,7 +319,7 @@
     pltpu.make_async_copy(everyone, everyone, gsend).wait()
 
 
-def stencil(src, dst, base, coef, hx_ref, hy_ref, hz_ref, lo, hi, y0, nk, nh, scale):
+def stencil(src, dst, base, coef, hx_ref, hy_ref, hz_ref, lo, hi, y0, nk, nh, scale, step):
     rk, rh, h0 = 8 * nk, 8 * nh, y0 - 1
     hr, hy_rows, kr, kl = pl.ds(h0, rh), pl.ds(y0, rh), pl.ds(y0, rk), pl.ds(h0, rk)
 
@@ -343,26 +343,28 @@
                 new = base[i, x, kr, :] + new
             dst[i, x, kr, :] = new
 
-    for i in range(-1, NP):
+    for i in range(-1, step):
         swirl(lo + i)
 
     def body(k, c):
-        x = jnp.minimum(lo + NP * k, hi - NP)
-        for i in range(NP):
+        x = jnp.minimum(lo + step * k, hi - step)
+        for i in range(step):
             relax(x + i)
-        for i in range(NP):
-            swirl(x + NP + i)
-        return c
-
-    lax.fori_loop(0, (hi - lo + NP - 1) // NP, body, 0)
-
-
-def relax_kernel(list_hbm, lap_ref, short_s, spot_s, many_s, coef_hbm, cond_hbm, field_hbm, out_ref,
-                 u, p, q, hx_ref, hy_ref, hz_ref, coef, cond, field, list_ref, spots, more, more_i, more_s, more_is, sems):
+        for i in range(step):
+            swirl(x + step + i)
+        return c
+
+    lax.fori_loop(0, (hi - lo + step - 1) // step, body, 0)
+
+
+def relax_kernel(list_hbm, lap_ref, short_hbm, spot_hbm, many_hbm, coef_hbm, cond_hbm, field_hbm, out_ref,
+                 u, p, q, hx_ref, hy_ref, hz_ref, short_s, spot_s, many_s, rows, coef, cond, field, list_ref, spots, more, more_i, more_s, more_is, sems):
     t = lax.axis_index("tile")
     loads = [pltpu.make_async_copy(a, b, sems.at[n])
              for n, (a, b) in enumerate(((coef_hbm, coef), (cond_hbm, cond), (field_hbm, field)))]
-    for copy in loads:
+    lists = [pltpu.make_async_copy(a, b, sems.at[n + 5])
+             for n, (a, b) in enumerate(((many_hbm, many_s), (spot_hbm, spot_s), (short_hbm, short_s)))]
+    for copy in lists + loads:
         copy.start()
 
     flat = u.reshape(3, PLANES * YR, 128)
@@ -374,6 +376,8 @@
 
     lax.fori_loop(0, PLANES, clear, 0)
     lane_id = iota((1, 128), 1)
+    for copy in lists:
+        copy.wait()
 
     def drop(k, most):
         for i in range(2):
@@ -463,13 +467,14 @@
         for i in range(3):
             src[i, B0 - 1] = pltpu.roll(src[i, B0 + RUN - 1], SEG, 1)
             src[i, B0 + RUN] = pltpu.roll(src[i, B0], 128 - SEG, 1)
-        stencil(src, dst, base, coef, hx_ref, hy_ref, hz_ref, B0, B0 + RUN, 8 - e, nk, nh, scale)
-        stencil(src, dst, base, coef, hx_ref, hy_ref, hz_ref, OWN - e, OWN + CX + e, 8 - e, nk, nh, scale)
+        stencil(src, dst, base, coef, hx_ref, hy_ref, hz_ref, B0, B0 + RUN, 8 - e, nk, nh, scale, NP_B)
+        stencil(src, dst, base, coef, hx_ref, hy_ref, hz_ref, OWN - e, OWN + CX + e, 8 - e, nk, nh, scale, NP_A)
 
     loads[1].wait()
     loads[2].wait()
     lane = iota((CY, 128), 1)
     own_y = pl.ds(8, CY)
+    leaving = []
     lap = lap_ref[0]
     for g in range(RUNS):
         begin, end = max(0, RUN * g - RIM), min(CX, RUN * (g + 1) - RIM)
@@ -483,10 +488,15 @@
                     value = jnp.where(lane >= CZ - 2 * RIM, pltpu.roll(rims, (ZB - SEG * g) % 128, 1),
                                       pltpu.roll(q[i, OWN + x, own_y, :], 128 - RIM, 1))
                     total = total + field[i, x].astype(F32) * value
-                out_ref[x] = -lap * cond[x] * total
+                rows[x] = -lap * cond[x] * total
             return c
 
         lax.fori_loop(0, (end - begin + 3) // 4, combine, 0)
+        made = pltpu.make_async_copy(rows.at[pl.ds(begin, end - begin)], out_ref.at[pl.ds(begin, end - begin)], sems.at[8 + g])
+        made.start()
+        leaving.append(made)
+    for made in leaving:
+        made.wait()
 
 
 def spread_kernel(part_ref, out_ref, send, recv, lsem):
@@ -514,6 +524,16 @@
     others = out_ref.at[pl.ds(0, 2 * TILES - 1)]
     for sem in (send, recv):
         pltpu.make_async_copy(others, others, sem).wait()
+
+
+def add_kernel(both_ref, out_ref):
+    def body(k, c):
+        done = [both_ref[8 * k + j] + both_ref[TILES + 8 * k + j] for j in range(8)]
+        for j in range(8):
+            out_ref[8 * k + j, 0] = done[j]
+        return c
+
+    lax.fori_loop(0, TILES // 8, body, 0)
 
 
 def local(residual, row_counts, recv_owner, recv_cell, conductivity, laplace, forward_field):
@@ -552,11 +572,16 @@
         relax_kernel,
         name="relax_tile",
         out_shape=jax.ShapeDtypeStruct((CX, CY, CZ), F32),
-        in_specs=[hbm(), smem, smem, smem, smem, hbm(), hbm(), hbm()],
-        out_specs=vmem(),
+        in_specs=[hbm(), smem, hbm(), hbm(), hbm(), hbm(), hbm(), hbm()],
+        out_specs=hbm(),
         scratch_shapes=[pltpu.VMEM((3, PLANES, YR, 128), F32)] * 3
-        + [pltpu.VMEM((PLANES, YR, 128), F32)] * 4
+        + [pltpu.VMEM((PLANES, YR, 128), F32)] * 3
         + [
+            pltpu.SMEM((104 * 128,), F32),
+            pltpu.SMEM((40 * 128,), I32),
+            pltpu.SMEM((8, 128), I32),
+            pltpu.VMEM((CX, CY, CZ), F32),
+            pltpu.VMEM((PLANES, YR, 128), F32),
             pltpu.VMEM((CX, CY, CZ), F32),
             pltpu.VMEM((3, CX, CY, CZ), BF16),
             pltpu.VMEM((TILES, 8, 128), F32),
@@ -565,7 +590,7 @@
             pltpu.VMEM((8, 128), I32),
             pltpu.SMEM((8, 128), F32),
             pltpu.SMEM((8, 128), I32),
-            pltpu.SemaphoreType.DMA((5,)),
+            pltpu.SemaphoreType.DMA((12,)),
         ],
         compiler_params=pltpu.CompilerParams(vmem_limit_bytes=62 * 2**20),
     )(lists, laplace, short.reshape(-1), spot.reshape(-1), many, coef, cond, forward_field[0, 0])
@@ -578,7 +603,13 @@
         scratch_shapes=[pltpu.SemaphoreType.DMA] * 3,
         compiler_params=pltpu.CompilerParams(collective_id=1, has_side_effects=True, vmem_limit_bytes=62 * 2**20),
     )(partial)
-    return (both[:TILES] + both[TILES:])[:, None]
+    return pl.pallas_call(
+        add_kernel,
+        name="add_frequencies",
+        out_shape=jax.ShapeDtypeStruct((TILES, 1, 16, CZ), F32),
+        in_specs=[vmem()],
+        out_specs=vmem(),
+    )(both)
 
 
 def solution(mesh):

time: 111 us -> 107 us (0.964); the launches traced: 113 us -> 106 us
  Pallas kernels: 110 us -> 106 us
  other arithmetic: 2.06 us -> 0 us
    pallas_call x1, Pallas kernels: 37.7 us -> 33.1 us  [local(): pl.pallas_call(spread_kernel, name='spread_rows', out_shape=jax.ShapeDtyp...]
    pallas_call x0 -> x1, Pallas kernels: none -> 2.09 us  [local(): pl.pallas_call(add_kernel, name='add_frequencies', out_shape=jax.ShapeDty...]
    broadcast_in_dim x1 -> x0, other arithmetic: 2.06 us -> none  [local(): return (both[:TILES] + both[TILES:])[:, None]]
    pallas_call x1, Pallas kernels: 41.4 us -> 39.6 us  [local(): pl.pallas_call(relax_kernel, name='relax_tile', out_shape=jax.ShapeDtypeS...]
where the time goes in v6:
time: 107 us; the launch traced here: 106 us
  Pallas kernels  106 us (99%)
    pallas_call x1, Pallas kernels, local(): pl.pallas_call(relax_kernel, name='relax_tile', out_shape=jax.ShapeDtypeS...  39.6 us
    pallas_call x1, Pallas kernels, local(): pl.pallas_call(spread_kernel, name='spread_rows', out_shape=jax.ShapeDtyp...  33.1 us
    pallas_call x1, Pallas kernels, local(): pl.pallas_call(gather_kernel, name='gather_lists', out_shape=(jax.ShapeDt...  30.8 us

profile of v6, /device:TPU:1, one launch (start us, length us, event | category | flops | bytes accessed | tf_op | source)
XLA Modules:
  0.0 106.3 jit_solution(14680646829879315539)
XLA Ops:
  0.7 30.8 %gather_lists.1 = (f32[64,8,128]{2,1,0:T(8,128)}, f32[112,56,128]{2,1,0:T(8,128)}, f32[104,128]{1,0:T(8,128)}, s32[40,128]{1,0:T(8,128)}, s32[8,128]{1,0:T(8,128)}) custom-call(f32[3,1,1024]{2,1,0:T(1,128)} %bitcast.12, s32[1,256]{1,0:T(1,128)} %cnt_hbm.1, s32[1,256]{1,0:T(1,128)} %bitcast.13, s32[1,256]{1,0:T(1,128)} %bitcast.14, f32[1]{0:T(128)S(6)} %copy.8.lap_ref, ...), custom_call_target="tpu_custom_call" | custom-call | tf_op jit(solution)/shard_map/gather_lists/pallas_call | solution.py:542
  31.5 39.6 %relax_tile.1.part_ref = f32[64,32,128]{2,1,0:T(8,128)} custom-call(f32[64,8,128]{2,1,0:T(8,128)} %get-tuple-element.10.list_hbm, f32[1]{0:T(128)S(6)} %copy.8.lap_ref, f32[13312]{0:T(1024)} %bitcast.10, s32[5120]{0:T(1024)} %bitcast.11, s32[8,128]{1,0:T(8,128)} %get-tuple-element.13.many_hbm, f32[112,56,128]{2,1,0:T(8,128)} %get-tuple-element.14.coef_hbm, ...), custom_call_target="tpu_custom_call" | custom-call | tf_op jit(solution)/shard_map/relax_tile/pallas_call | solution.py:571
  71.1 33.1 %spread_rows.1.both_ref = f32[128,16,128]{2,1,0:T(8,128)} custom-call(f32[64,32,128]{2,1,0:T(8,128)} %relax_tile.1.part_ref), custom_call_target="tpu_custom_call" | custom-call | tf_op jit(solution)/shard_map/spread_rows/pallas_call | solution.py:597
  104.2 2.1 %add_frequencies.1 = f32[64,1,16,128]{3,2,1,0:T(8,128)} custom-call(f32[128,16,128]{2,1,0:T(8,128)} %spread_rows.1.both_ref), custom_call_target="tpu_custom_call" | custom-call | tf_op jit(solution)/shard_map/add_frequencies/pallas_call | solution.py:606

commit v7 on v6

--- a/solution.py
+++ b/solution.py
@@ -18,7 +18,7 @@
 NP_A, NP_B = 8, 10
 RIM = 7
 
-YR = 56
+YR = 64
 B0 = 81
 RUN = 20
 SEG = 28
@@ -97,8 +97,8 @@
     return (got[0:4] + got[4:8]) + got[8:12]
 
 
-def gather_kernel(res_hbm, cnt_hbm, tile_hbm, cell_hbm, lap_ref, cond_ref, list_ref, coef_ref, short_ref, spot_ref, many_ref,
-                  res_ref, cnt_ref, tile_ref, cell_ref, spots, raw, cext, pack, low, high, sends, recvs, zsend, zrecv, gsend, grecv, lsem):
+def gather_kernel(res_hbm, cnt_hbm, tile_hbm, cell_hbm, lap_ref, cond_ref, list_ref, coef_hbm, short_ref, spot_ref, many_ref,
+                  res_ref, cnt_ref, tile_ref, cell_ref, spots, raw, cext, pack, low, high, sends, recvs, zsend, zrecv, gsend, grecv, lsem, coef_ref):
     f, t = lax.axis_index("freq"), lax.axis_index("tile")
     me = f * TILES + t
     tx, ty, tz = place(t)
@@ -282,6 +282,10 @@
 
         lax.fori_loop(0, 10, patch, 0)
 
+    leaving = [pltpu.make_async_copy(coef_ref.at[pl.ds(b, n)], coef_hbm.at[pl.ds(b, n)], lsem.at[5 + k])
+               for k, (b, n) in enumerate(((0, 80), (80, 24)))]
+    leaving[0].start()
+
     @pl.when(tz < TZ - 1)
     def _():
         rim(0).wait_recv()
@@ -303,6 +307,8 @@
 
         lax.fori_loop(0, RUN // 2, patch, 0)
 
+    leaving[1].start()
+
     for n, (dx, dy) in enumerate(ways):
         @pl.when(inside(dx, dy))
         def _(n=n):
@@ -317,6 +323,8 @@
         rim(0).wait_send()
 
     pltpu.make_async_copy(everyone, everyone, gsend).wait()
+    for copy in leaving:
+        copy.wait()
 
 
 def stencil(src, dst, base, coef, hx_ref, hy_ref, hz_ref, lo, hi, y0, nk, nh, scale, step):
@@ -361,7 +369,7 @@
                  u, p, q, hx_ref, hy_ref, hz_ref, short_s, spot_s, many_s, rows, coef, cond, field, list_ref, spots, more, more_i, more_s, more_is, sems):
     t = lax.axis_index("tile")
     loads = [pltpu.make_async_copy(a, b, sems.at[n])
-             for n, (a, b) in enumerate(((coef_hbm, coef), (cond_hbm, cond), (field_hbm, field)))]
+             for n, (a, b) in enumerate(((coef_hbm.at[pl.ds(0, 104)], coef.at[pl.ds(0, 104)]), (cond_hbm, cond), (field_hbm, field)))]
     lists = [pltpu.make_async_copy(a, b, sems.at[n + 5])
              for n, (a, b) in enumerate(((many_hbm, many_s), (spot_hbm, spot_s), (short_hbm, short_s)))]
     for copy in lists + loads:
@@ -505,7 +513,7 @@
     barrier = pltpu.get_barrier_semaphore()
 
     def greet(i, c):
-        pl.semaphore_signal(barrier, inc=1, device_id=me ^ i, device_id_type=pl.DeviceIdType.LOGICAL)
+        pl.semaphore_signal(barrier, inc=1, device_id=me ^ (2 * TILES - i), device_id_type=pl.DeviceIdType.LOGICAL)
         return c
 
     lax.fori_loop(1, 2 * TILES, greet, 0)
@@ -514,7 +522,7 @@
     pl.semaphore_wait(barrier, 2 * TILES - 1)
 
     def share(i, c):
-        d = me ^ i
+        d = me ^ (2 * TILES - i)
         pltpu.make_async_remote_copy(part_ref.at[d & (TILES - 1), pl.ds((d >> 6) * 16, 16)], out_ref.at[me], send, recv,
                                      device_id=d, device_id_type=pl.DeviceIdType.LOGICAL).start()
         return c
@@ -526,7 +534,11 @@
         pltpu.make_async_copy(others, others, sem).wait()
 
 
-def add_kernel(both_ref, out_ref):
+def add_kernel(both_hbm, out_ref, both_ref, sem):
+    load = pltpu.make_async_copy(both_hbm, both_ref, sem)
+    load.start()
+    load.wait()
+
     def body(k, c):
         done = [both_ref[8 * k + j] + both_ref[TILES + 8 * k + j] for j in range(8)]
         for j in range(8):
@@ -546,7 +558,7 @@
                    jax.ShapeDtypeStruct((104, 128), F32), jax.ShapeDtypeStruct((40, 128), I32),
                    jax.ShapeDtypeStruct((8, 128), I32)),
         in_specs=[hbm(), hbm(), hbm(), hbm(), smem, hbm()],
-        out_specs=(vmem(), vmem(), vmem(), vmem(), vmem()),
+        out_specs=(vmem(), hbm(), vmem(), vmem(), vmem()),
         scratch_shapes=[
             pltpu.VMEM((3, 1, 1024), F32),
             pltpu.VMEM((1, 256), I32),
@@ -564,7 +576,8 @@
             pltpu.SemaphoreType.DMA((2,)),
             pltpu.SemaphoreType.DMA,
             pltpu.SemaphoreType.DMA,
-            pltpu.SemaphoreType.DMA((5,)),
+            pltpu.SemaphoreType.DMA((7,)),
+            pltpu.VMEM((PLANES, YR, 128), F32),
         ],
         compiler_params=pltpu.CompilerParams(collective_id=0, has_side_effects=True, vmem_limit_bytes=62 * 2**20),
     )(residual.transpose(1, 0, 2), row_counts, recv_owner.reshape(1, -1), recv_cell.reshape(1, -1), laplace, cond)
@@ -601,14 +614,16 @@
         in_specs=[hbm()],
         out_specs=hbm(),
         scratch_shapes=[pltpu.SemaphoreType.DMA] * 3,
-        compiler_params=pltpu.CompilerParams(collective_id=1, has_side_effects=True, vmem_limit_bytes=62 * 2**20),
+        compiler_params=pltpu.CompilerParams(collective_id=1, has_side_effects=True, vmem_limit_bytes=4 * 2**20),
     )(partial)
     return pl.pallas_call(
         add_kernel,
         name="add_frequencies",
         out_shape=jax.ShapeDtypeStruct((TILES, 1, 16, CZ), F32),
-        in_specs=[vmem()],
+        in_specs=[hbm()],
         out_specs=vmem(),
+        scratch_shapes=[pltpu.VMEM((2 * TILES, 16, CZ), F32), pltpu.SemaphoreType.DMA],
+        compiler_params=pltpu.CompilerParams(vmem_limit_bytes=4 * 2**20),
     )(both)
 
 

time: 107 us -> 105 us (0.981)
  Pallas kernels: 106 us -> 103 us
  local copies, waits for them, and re-layouts: 0 us -> 1.22 us
    unnamed x0 -> x2, local copies, waits for them, and re-layouts: none -> 1.22 us
    pallas_call x1, Pallas kernels: 2.09 us -> 0.96 us  [local(): pl.pallas_call(add_kernel, name='add_frequencies', out_shape=jax.ShapeDty...]
where the time goes in v7:
time: 105 us
  Pallas kernels  103 us (98%)
  local copies, waits for them, and re-layouts  1.22 us (1%)
    pallas_call x1, Pallas kernels, local(): pl.pallas_call(relax_kernel, name='relax_tile', out_shape=jax.ShapeDtypeS...  38.9 us
    pallas_call x1, Pallas kernels, local(): pl.pallas_call(spread_kernel, name='spread_rows', out_shape=jax.ShapeDtyp...  32.9 us
    pallas_call x1, Pallas kernels, local(): pl.pallas_call(gather_kernel, name='gather_lists', out_shape=(jax.ShapeDt...  30.6 us

profile of v7, /device:TPU:1, one launch (start us, length us, event | category | flops | bytes accessed | tf_op | source)
XLA Modules:
  0.0 105.2 jit_solution(14956478720142224186)
XLA Ops:
  0.7 30.6 %gather_lists.1 = (f32[64,8,128]{2,1,0:T(8,128)}, f32[112,64,128]{2,1,0:T(8,128)}, f32[104,128]{1,0:T(8,128)}, s32[40,128]{1,0:T(8,128)}, s32[8,128]{1,0:T(8,128)}) custom-call(f32[3,1,1024]{2,1,0:T(1,128)} %bitcast.12, s32[1,256]{1,0:T(1,128)} %cnt_hbm.1, s32[1,256]{1,0:T(1,128)} %bitcast.13, s32[1,256]{1,0:T(1,128)} %bitcast.14, f32[1]{0:T(128)S(6)} %copy.8.lap_ref, ...), custom_call_target="tpu_custom_call" | custom-call | tf_op jit(solution)/shard_map/gather_lists/pallas_call | solution.py:554
  31.3 38.9 %relax_tile.1.part_ref = f32[64,32,128]{2,1,0:T(8,128)} custom-call(f32[64,8,128]{2,1,0:T(8,128)} %get-tuple-element.10.list_hbm, f32[1]{0:T(128)S(6)} %copy.8.lap_ref, f32[13312]{0:T(1024)} %bitcast.10, s32[5120]{0:T(1024)} %bitcast.11, s32[8,128]{1,0:T(8,128)} %get-tuple-element.13.many_hbm, f32[112,64,128]{2,1,0:T(8,128)} %get-tuple-element.14.coef_hbm, ...), custom_call_target="tpu_custom_call" | custom-call | tf_op jit(solution)/shard_map/relax_tile/pallas_call | solution.py:584
  70.2 0.0 copy-start
  70.2 1.2 %copy-done = f32[64,32,128]{2,1,0:T(8,128)S(1)} copy-done((f32[64,32,128]{2,1,0:T(8,128)S(1)}, f32[64,32,128]{2,1,0:T(8,128)}, u32[]{:S(2)}) %copy-start) | copy-done | bytes 1048600
  71.4 32.9 %spread_rows.1.both_hbm = f32[128,16,128]{2,1,0:T(8,128)S(1)} custom-call(f32[64,32,128]{2,1,0:T(8,128)S(1)} %copy-done), custom_call_target="tpu_custom_call" | custom-call | tf_op jit(solution)/shard_map/spread_rows/pallas_call | solution.py:610
  104.3 1.0 add_frequencies.1
Async XLA Ops:
  70.2 1.2 %copy-start = (f32[64,32,128]{2,1,0:T(8,128)S(1)}, f32[64,32,128]{2,1,0:T(8,128)}, u32[]{:S(2)}) copy-start(f32[64,32,128]{2,1,0:T(8,128)} %relax_tile.1.part_ref) | copy-start | bytes 3145732

commit v8 on v7

--- a/solution.py
+++ b/solution.py
@@ -507,7 +507,7 @@
         made.wait()
 
 
-def spread_kernel(part_ref, out_ref, send, recv, lsem):
+def spread_kernel(part_ref, out_ref, got, send, recv, lsem):
     f, t = lax.axis_index("freq"), lax.axis_index("tile")
     me = f * TILES + t
     barrier = pltpu.get_barrier_semaphore()
@@ -517,35 +517,29 @@
         return c
 
     lax.fori_loop(1, 2 * TILES, greet, 0)
-    mine = pltpu.make_async_copy(part_ref.at[t, pl.ds(f * 16, 16)], out_ref.at[me], lsem)
+    mine = pltpu.make_async_copy(part_ref.at[t, pl.ds(f * 16, 16)], got.at[me], lsem)
     mine.start()
     pl.semaphore_wait(barrier, 2 * TILES - 1)
 
     def share(i, c):
         d = me ^ (2 * TILES - i)
-        pltpu.make_async_remote_copy(part_ref.at[d & (TILES - 1), pl.ds((d >> 6) * 16, 16)], out_ref.at[me], send, recv,
+        pltpu.make_async_remote_copy(part_ref.at[d & (TILES - 1), pl.ds((d >> 6) * 16, 16)], got.at[me], send, recv,
                                      device_id=d, device_id_type=pl.DeviceIdType.LOGICAL).start()
         return c
 
     lax.fori_loop(1, 2 * TILES, share, 0)
     mine.wait()
-    others = out_ref.at[pl.ds(0, 2 * TILES - 1)]
+    others = got.at[pl.ds(0, 2 * TILES - 1)]
     for sem in (send, recv):
         pltpu.make_async_copy(others, others, sem).wait()
 
-
-def add_kernel(both_hbm, out_ref, both_ref, sem):
-    load = pltpu.make_async_copy(both_hbm, both_ref, sem)
-    load.start()
-    load.wait()
-
-    def body(k, c):
-        done = [both_ref[8 * k + j] + both_ref[TILES + 8 * k + j] for j in range(8)]
+    def add(k, c):
+        done = [got[8 * k + j] + got[TILES + 8 * k + j] for j in range(8)]
         for j in range(8):
             out_ref[8 * k + j, 0] = done[j]
         return c
 
-    lax.fori_loop(0, TILES // 8, body, 0)
+    lax.fori_loop(0, TILES // 8, add, 0)
 
 
 def local(residual, row_counts, recv_owner, recv_cell, conductivity, laplace, forward_field):
@@ -607,24 +601,15 @@
         ],
         compiler_params=pltpu.CompilerParams(vmem_limit_bytes=62 * 2**20),
     )(lists, laplace, short.reshape(-1), spot.reshape(-1), many, coef, cond, forward_field[0, 0])
-    both = pl.pallas_call(
+    return pl.pallas_call(
         spread_kernel,
         name="spread_rows",
-        out_shape=jax.ShapeDtypeStruct((2 * TILES, 16, CZ), F32),
-        in_specs=[hbm()],
-        out_specs=hbm(),
-        scratch_shapes=[pltpu.SemaphoreType.DMA] * 3,
-        compiler_params=pltpu.CompilerParams(collective_id=1, has_side_effects=True, vmem_limit_bytes=4 * 2**20),
-    )(partial)
-    return pl.pallas_call(
-        add_kernel,
-        name="add_frequencies",
         out_shape=jax.ShapeDtypeStruct((TILES, 1, 16, CZ), F32),
         in_specs=[hbm()],
         out_specs=vmem(),
-        scratch_shapes=[pltpu.VMEM((2 * TILES, 16, CZ), F32), pltpu.SemaphoreType.DMA],
-        compiler_params=pltpu.CompilerParams(vmem_limit_bytes=4 * 2**20),
-    )(both)
+        scratch_shapes=[pltpu.VMEM((2 * TILES, 16, CZ), F32)] + [pltpu.SemaphoreType.DMA] * 3,
+        compiler_params=pltpu.CompilerParams(collective_id=1, has_side_effects=True, vmem_limit_bytes=63 * 2**20),
+    )(partial)
 
 
 def solution(mesh):

time: 105 us -> 107 us (1.019); the launches traced: 105 us -> 106 us
    pallas_call x1, Pallas kernels: 32.9 us -> 34.6 us  [local(): pl.pallas_call(spread_kernel, name='spread_rows', out_shape=jax.ShapeDtyp...]
where the time goes in v8:
time: 107 us; the launch traced here: 106 us
  Pallas kernels  103 us (96%)
  local copies, waits for them, and re-layouts  1.87 us (2%)
    pallas_call x1, Pallas kernels, local(): pl.pallas_call(relax_kernel, name='relax_tile', out_shape=jax.ShapeDtypeS...  38 us
    pallas_call x1, Pallas kernels, local(): pl.pallas_call(spread_kernel, name='spread_rows', out_shape=jax.ShapeDtyp...  34.6 us
    pallas_call x1, Pallas kernels, local(): pl.pallas_call(gather_kernel, name='gather_lists', out_shape=(jax.ShapeDt...  30.6 us

profile of v8, /device:TPU:1, one launch (start us, length us, event | category | flops | bytes accessed | tf_op | source)
XLA Modules:
  0.0 105.8 jit_solution(3755273707224150317)
XLA Ops:
  0.7 30.6 %gather_lists.1 = (f32[64,8,128]{2,1,0:T(8,128)}, f32[112,64,128]{2,1,0:T(8,128)}, f32[104,128]{1,0:T(8,128)}, s32[40,128]{1,0:T(8,128)}, s32[8,128]{1,0:T(8,128)}) custom-call(f32[3,1,1024]{2,1,0:T(1,128)} %bitcast.12, s32[1,256]{1,0:T(1,128)} %cnt_hbm.1, s32[1,256]{1,0:T(1,128)} %bitcast.13, s32[1,256]{1,0:T(1,128)} %bitcast.14, f32[1]{0:T(128)S(6)} %copy.9.lap_ref, ...), custom_call_target="tpu_custom_call" | custom-call | tf_op jit(solution)/shard_map/gather_lists/pallas_call | solution.py:548
  31.3 38.0 %relax_tile.1.part_ref = f32[64,32,128]{2,1,0:T(8,128)} custom-call(f32[64,8,128]{2,1,0:T(8,128)} %get-tuple-element.10.list_hbm, f32[1]{0:T(128)S(6)} %copy.9.lap_ref, f32[13312]{0:T(1024)} %bitcast.10, s32[5120]{0:T(1024)} %bitcast.11, s32[8,128]{1,0:T(8,128)} %get-tuple-element.13.many_hbm, f32[112,64,128]{2,1,0:T(8,128)} %get-tuple-element.14.coef_hbm, ...), custom_call_target="tpu_custom_call" | custom-call | tf_op jit(solution)/shard_map/relax_tile/pallas_call | solution.py:578
  69.3 34.6 %spread_rows.1 = f32[64,1,16,128]{3,2,1,0:T(8,128)} custom-call(f32[64,32,128]{2,1,0:T(8,128)} %relax_tile.1.part_ref), custom_call_target="tpu_custom_call" | custom-call | tf_op jit(solution)/shard_map/spread_rows/pallas_call | solution.py:604
  103.9 1.9 %copy.10 = f32[64,1,16,128]{3,2,1,0:T(8,128)} copy(f32[64,1,16,128]{3,2,1,0:T(8,128)} %spread_rows.1) | data formatting | bytes 1048576

commit v9 on v7

--- a/solution.py
+++ b/solution.py
@@ -488,8 +488,8 @@
         begin, end = max(0, RUN * g - RIM), min(CX, RUN * (g + 1) - RIM)
 
         def combine(k, c, g=g, begin=begin, end=end):
-            for j in range(4):
-                x = jnp.minimum(begin + 4 * k + j, end - 1)
+            for j in range(7):
+                x = jnp.minimum(begin + 7 * k + j, end - 1)
                 total = jnp.zeros((CY, 128), F32)
                 for i in range(3):
                     rims = q[i, B0 + x + RIM - RUN * g, own_y, :]
@@ -499,7 +499,7 @@
                 rows[x] = -lap * cond[x] * total
             return c
 
-        lax.fori_loop(0, (end - begin + 3) // 4, combine, 0)
+        lax.fori_loop(0, (end - begin + 6) // 7, combine, 0)
         made = pltpu.make_async_copy(rows.at[pl.ds(begin, end - begin)], out_ref.at[pl.ds(begin, end - begin)], sems.at[8 + g])
         made.start()
         leaving.append(made)

time: 105 us -> 104 us (level)
  no operation moved by 1% of the time
where the time goes in v9:
time: 104 us; the launch traced here: 105 us
  Pallas kernels  103 us (99%)
  local copies, waits for them, and re-layouts  1.22 us (1%)
    pallas_call x1, Pallas kernels, local(): pl.pallas_call(relax_kernel, name='relax_tile', out_shape=jax.ShapeDtypeS...  38.8 us
    pallas_call x1, Pallas kernels, local(): pl.pallas_call(spread_kernel, name='spread_rows', out_shape=jax.ShapeDtyp...  32.7 us
    pallas_call x1, Pallas kernels, local(): pl.pallas_call(gather_kernel, name='gather_lists', out_shape=(jax.ShapeDt...  30.6 us

profile of v9, /device:TPU:1, one launch (start us, length us, event | category | flops | bytes accessed | tf_op | source)
XLA Modules:
  0.0 104.9 jit_solution(3853123824556024387)
XLA Ops:
  0.7 30.6 %gather_lists.1 = (f32[64,8,128]{2,1,0:T(8,128)}, f32[112,64,128]{2,1,0:T(8,128)}, f32[104,128]{1,0:T(8,128)}, s32[40,128]{1,0:T(8,128)}, s32[8,128]{1,0:T(8,128)}) custom-call(f32[3,1,1024]{2,1,0:T(1,128)} %bitcast.12, s32[1,256]{1,0:T(1,128)} %cnt_hbm.1, s32[1,256]{1,0:T(1,128)} %bitcast.13, s32[1,256]{1,0:T(1,128)} %bitcast.14, f32[1]{0:T(128)S(6)} %copy.8.lap_ref, ...), custom_call_target="tpu_custom_call" | custom-call | tf_op jit(solution)/shard_map/gather_lists/pallas_call | solution.py:554
  31.3 38.8 %relax_tile.1.part_ref = f32[64,32,128]{2,1,0:T(8,128)} custom-call(f32[64,8,128]{2,1,0:T(8,128)} %get-tuple-element.10.list_hbm, f32[1]{0:T(128)S(6)} %copy.8.lap_ref, f32[13312]{0:T(1024)} %bitcast.10, s32[5120]{0:T(1024)} %bitcast.11, s32[8,128]{1,0:T(8,128)} %get-tuple-element.13.many_hbm, f32[112,64,128]{2,1,0:T(8,128)} %get-tuple-element.14.coef_hbm, ...), custom_call_target="tpu_custom_call" | custom-call | tf_op jit(solution)/shard_map/relax_tile/pallas_call | solution.py:584
  70.1 0.0 copy-start
  70.1 1.2 %copy-done = f32[64,32,128]{2,1,0:T(8,128)S(1)} copy-done((f32[64,32,128]{2,1,0:T(8,128)S(1)}, f32[64,32,128]{2,1,0:T(8,128)}, u32[]{:S(2)}) %copy-start) | copy-done | bytes 1048600
  71.3 32.7 %spread_rows.1.both_hbm = f32[128,16,128]{2,1,0:T(8,128)S(1)} custom-call(f32[64,32,128]{2,1,0:T(8,128)S(1)} %copy-done), custom_call_target="tpu_custom_call" | custom-call | tf_op jit(solution)/shard_map/spread_rows/pallas_call | solution.py:610
  104.0 1.0 add_frequencies.1
Async XLA Ops:
  70.1 1.2 %copy-start = (f32[64,32,128]{2,1,0:T(8,128)S(1)}, f32[64,32,128]{2,1,0:T(8,128)}, u32[]{:S(2)}) copy-start(f32[64,32,128]{2,1,0:T(8,128)} %relax_tile.1.part_ref) | copy-start | bytes 3145732
